TPU v7x, 32 devices: a whole 2x2x4 slice. The times are simulated.
32 devices in a mesh: dp: 4 (over y, x), seq: 8 (over z, core).
Axes of the slice: x: 2, y: 2, z: 4, core: 2. Of those that a mesh axis runs over, the one named last changes fastest.
Arguments:
- inputs: bfloat16 [8, 1024, 1024], P('dp', 'seq'), may hold values from -6 to 6
- memory: bfloat16 [8, 512, 1024], P('dp', 'seq'), may hold values from -6 to 6
- mem_lengths: int32 [8], P('dp'), may hold values from 64 to 512, as said below
- cross_mask: int32 [8, 512], P('dp'), may hold values from 0 to 1, as said below
- buckets: int32 [1024], replicated, may hold values from 0 to 31
- self_query: bfloat16 [1024, 1024], P(('dp', 'seq')), may hold values from -0.1875 to 0.1875
- self_key: bfloat16 [1024, 512], P(('dp', 'seq')), may hold values from -0.1875 to 0.1875
- self_value: bfloat16 [1024, 512], P(('dp', 'seq')), may hold values from -0.1875 to 0.1875
- self_output: bfloat16 [1024, 1024], P(('dp', 'seq')), may hold values from -1.5 to 1.5
- cross_query: bfloat16 [1024, 1024], P(('dp', 'seq')), may hold values from -0.1875 to 0.1875
- cross_key: bfloat16 [1024, 512], P(('dp', 'seq')), may hold values from -0.1875 to 0.1875
- cross_value: bfloat16 [1024, 512], P(('dp', 'seq')), may hold values from -0.1875 to 0.1875
- cross_output: bfloat16 [1024, 1024], P(('dp', 'seq')), may hold values from -1 to 1
- gate_weight: bfloat16 [1024, 2816], P(('dp', 'seq')), may hold values from -0.1875 to 0.1875
- up_weight: bfloat16 [1024, 2816], P(('dp', 'seq')), may hold values from -0.1875 to 0.1875
- down_weight: bfloat16 [2816, 1024], P(('dp', 'seq')), may hold values from -0.15625 to 0.15625
- self_gain: bfloat16 [1024], P(('dp', 'seq')), may hold values from 0.5 to 1.5
- cross_gain: bfloat16 [1024], P(('dp', 'seq')), may hold values from 0.5 to 1.5
- feed_gain: bfloat16 [1024], P(('dp', 'seq')), may hold values from 0.5 to 1.5
- position_bias: bfloat16 [512], P(('dp', 'seq')), may hold values from -4 to 4
- cotangent: bfloat16 [8, 1024, 1024], P('dp', 'seq'), may hold values from -6 to 6
Outputs:
- output: bfloat16 [8, 1024, 1024], P('dp', 'seq')
- input_grad: float32 [8, 1024, 1024], P('dp', 'seq')
- memory_grad: float32 [8, 512, 1024], P('dp', 'seq')
- self_query_grad: float32 [1024, 1024], P(('dp', 'seq'))
- self_key_grad: float32 [1024, 512], P(('dp', 'seq'))
- self_value_grad: float32 [1024, 512], P(('dp', 'seq'))
- self_output_grad: float32 [1024, 1024], P(('dp', 'seq'))
- cross_query_grad: float32 [1024, 1024], P(('dp', 'seq'))
- cross_key_grad: float32 [1024, 512], P(('dp', 'seq'))
- cross_value_grad: float32 [1024, 512], P(('dp', 'seq'))
- cross_output_grad: float32 [1024, 1024], P(('dp', 'seq'))
- gate_weight_grad: float32 [1024, 2816], P(('dp', 'seq'))
- up_weight_grad: float32 [1024, 2816], P(('dp', 'seq'))
- down_weight_grad: float32 [2816, 1024], P(('dp', 'seq'))
- self_gain_grad: float32 [1024], P(('dp', 'seq'))
- cross_gain_grad: float32 [1024], P(('dp', 'seq'))
- feed_gain_grad: float32 [1024], P(('dp', 'seq'))
- position_bias_grad: float32 [512], P(('dp', 'seq'))
Inputs may be any that keep to these rules, and one draw needn't show every extreme that they name: mem_lengths[s] counts the leading memory rows of sequence s that exist; one sequence has exactly 512 rows and one exactly 64. cross_mask[s, 0] is 1 for every sequence.
All inputs are finite; a program needn't handle non-finite values.
Results may differ from a plain program's by a relative error of at most 0.025.
Values may be sent and summed in bfloat16 or wider, within the bound.
No kernel may reach another device: no remote copies, remote signals or barrier semaphores. Data moves between devices by JAX's collectives and lax.ppermute only.
A program may use at most 192 MiB of HBM per device.

v0:
```python
import jax
import jax.numpy as jnp
from jax import lax
from jax.sharding import PartitionSpec as P

H = 16
HD = 64
NB = 32
G = 8


epsilon = 1e-06
highest = lax.Precision.HIGHEST
masked_out = -1e30


def rms_scale(stream, norm_gain):
    return (
        stream * lax.rsqrt(jnp.mean(stream * stream, axis=-1, keepdims=True) + epsilon) * norm_gain
    )


def gated_unit(gate_value, lift_value):
    return jax.nn.gelu(gate_value, approximate=True) * lift_value


def project(left, right):
    return jnp.dot(left, right, preferred_element_type=jnp.float32)


def project_back(left, right):
    return jnp.einsum("spn,dn->spd", left, right, preferred_element_type=jnp.float32)


def weight_grad(left, right):
    return jnp.einsum("spa,spb->ab", left, right, preferred_element_type=jnp.float32)


def logits_of(queries, key_heads, position_terms, allowed, scaling):
    scores = (
        jnp.einsum("spgrd,slgd->sgrpl", queries, key_heads, preferred_element_type=jnp.float32)
        * scaling
    )
    return jnp.where(allowed, scores + position_terms, masked_out)


def softmax_rows(logits):
    peak = jnp.max(logits, axis=-1, keepdims=True)
    exps = jnp.exp(logits - peak)
    totals = jnp.sum(exps, axis=-1, keepdims=True)
    return (exps / totals, peak + jnp.log(totals))


def attention_back(attn_probs, queries, key_heads, value_heads, grad_out, scaling):
    grad_probs = jnp.einsum(
        "spgrd,slgd->sgrpl", grad_out, value_heads, preferred_element_type=jnp.float32
    )
    grad_logits = attn_probs * (
        grad_probs - jnp.sum(attn_probs * grad_probs, axis=-1, keepdims=True)
    )
    low_logits = grad_logits.astype(jnp.bfloat16)
    grad_query = (
        jnp.einsum("sgrpl,slgd->spgrd", low_logits, key_heads, preferred_element_type=jnp.float32)
        * scaling
    )
    grad_key = (
        jnp.einsum("sgrpl,spgrd->slgd", low_logits, queries, preferred_element_type=jnp.float32)
        * scaling
    )
    grad_value = jnp.einsum(
        "sgrpl,spgrd->slgd",
        attn_probs.astype(jnp.bfloat16),
        grad_out,
        preferred_element_type=jnp.float32,
    )
    return (grad_logits, grad_query, grad_key, grad_value)


def shards(
    inputs,
    memory,
    mem_lengths,
    cross_mask,
    buckets,
    self_query,
    self_key,
    self_value,
    self_output,
    cross_query,
    cross_key,
    cross_value,
    cross_output,
    gate_weight,
    up_weight,
    down_weight,
    self_gain,
    cross_gain,
    feed_gain,
    position_bias,
    cotangent,
):
    local_span = inputs.shape[1]
    mem_span = memory.shape[1]
    seq_count = lax.axis_size("seq")
    seq_index = lax.axis_index("seq")
    full_length = local_span * seq_count
    mem_total = mem_span * seq_count
    per_group = H // G
    kv_width = G * HD
    scaling = HD ** (-0.5)
    weight_shards = (
        self_query,
        self_key,
        self_value,
        self_output,
        cross_query,
        cross_key,
        cross_value,
        cross_output,
        gate_weight,
        up_weight,
        down_weight,
        self_gain,
        cross_gain,
        feed_gain,
        position_bias,
    )
    query_pos = seq_index * local_span + jnp.arange(local_span, dtype=jnp.int32)
    key_pos = jnp.arange(full_length, dtype=jnp.int32)
    distance = query_pos[:, None] - key_pos[None, :]
    causal = distance >= 0
    bucket_index = jnp.take(buckets, jnp.clip(distance, 0, full_length - 1))
    one_hot = (bucket_index[None, :, :] == jnp.arange(NB, dtype=jnp.int32)[:, None, None]).astype(
        jnp.bfloat16
    )
    mem_rows = jnp.arange(mem_total, dtype=jnp.int32)

    def micro(element):
        seq_in, mem_in, length_in, mask_in, cot_in = element
        seq_rows = seq_in[None]
        mem_block = mem_in[None]
        forward_weights = (
            lax.all_gather(weight_shards[0], ("dp", "seq"), axis=0, tiled=True),
            lax.all_gather(weight_shards[1], ("dp", "seq"), axis=0, tiled=True),
            lax.all_gather(weight_shards[2], ("dp", "seq"), axis=0, tiled=True),
            lax.all_gather(weight_shards[3], ("dp", "seq"), axis=0, tiled=True),
            lax.all_gather(weight_shards[4], ("dp", "seq"), axis=0, tiled=True),
            lax.all_gather(weight_shards[5], ("dp", "seq"), axis=0, tiled=True),
            lax.all_gather(weight_shards[6], ("dp", "seq"), axis=0, tiled=True),
            lax.all_gather(weight_shards[7], ("dp", "seq"), axis=0, tiled=True),
            lax.all_gather(weight_shards[8], ("dp", "seq"), axis=0, tiled=True),
            lax.all_gather(weight_shards[9], ("dp", "seq"), axis=0, tiled=True),
            lax.all_gather(weight_shards[10], ("dp", "seq"), axis=0, tiled=True),
            lax.all_gather(weight_shards[11], ("dp", "seq"), axis=0, tiled=True),
            lax.all_gather(weight_shards[12], ("dp", "seq"), axis=0, tiled=True),
            lax.all_gather(weight_shards[13], ("dp", "seq"), axis=0, tiled=True),
            lax.all_gather(weight_shards[14], ("dp", "seq"), axis=0, tiled=True),
        )
        (
            query_self,
            key_self,
            value_self,
            output_self,
            query_cross,
            key_cross,
            value_cross,
            output_cross,
            gate_full,
            lift_full,
            down_full,
            gain_first,
            gain_second,
            gain_third,
            bias_table,
        ) = forward_weights
        stream = seq_rows.astype(jnp.float32)
        act_first = rms_scale(stream, gain_first.astype(jnp.float32)).astype(jnp.bfloat16)
        queries = project(act_first, query_self).astype(jnp.bfloat16)
        local_kv = project(act_first, jnp.concatenate([key_self, value_self], axis=1)).astype(
            jnp.bfloat16
        )
        memory_kv = project(mem_block, jnp.concatenate([key_cross, value_cross], axis=1)).astype(
            jnp.bfloat16
        )
        full_kv, full_memory_kv = (
            lax.all_gather(local_kv, "seq", axis=1, tiled=True),
            lax.all_gather(memory_kv, "seq", axis=1, tiled=True),
        )
        self_bias = jnp.einsum(
            "bpl,bh->hpl", one_hot, bias_table.reshape(NB, H), preferred_element_type=jnp.float32
        ).reshape(G, per_group, local_span, full_length)
        query_heads = queries.reshape(1, local_span, G, per_group, HD)
        self_keys = full_kv[..., :kv_width].reshape(1, full_length, G, HD)
        self_values = full_kv[..., kv_width:].reshape(1, full_length, G, HD)
        self_probs, self_lse = softmax_rows(
            logits_of(query_heads, self_keys, self_bias, causal, scaling)
        )
        self_att = jnp.einsum(
            "sgrpl,slgd->spgrd",
            self_probs.astype(jnp.bfloat16),
            self_values,
            preferred_element_type=jnp.float32,
        ).reshape(1, local_span, H * HD)
        self_att = self_att.astype(jnp.bfloat16)
        stream_one = stream + project(self_att, output_self)
        usable = (mask_in > 0) & (mem_rows < length_in)
        cross_allowed = usable[None, None, None, None, :]
        act_second = rms_scale(stream_one, gain_second.astype(jnp.float32)).astype(jnp.bfloat16)
        cross_queries = (
            project(act_second, query_cross)
            .astype(jnp.bfloat16)
            .reshape(1, local_span, G, per_group, HD)
        )
        cross_keys = full_memory_kv[..., :kv_width].reshape(1, mem_total, G, HD)
        cross_values = full_memory_kv[..., kv_width:].reshape(1, mem_total, G, HD)
        cross_probs, cross_lse = softmax_rows(
            logits_of(cross_queries, cross_keys, 0.0, cross_allowed, scaling)
        )
        cross_att = jnp.einsum(
            "sgrpl,slgd->spgrd",
            cross_probs.astype(jnp.bfloat16),
            cross_values,
            preferred_element_type=jnp.float32,
        ).reshape(1, local_span, H * HD)
        cross_att = cross_att.astype(jnp.bfloat16)
        stream_two = stream_one + project(cross_att, output_cross)
        act_third = rms_scale(stream_two, gain_third.astype(jnp.float32)).astype(jnp.bfloat16)
        gate_value = project(act_third, gate_full)
        lift_value = project(act_third, lift_full)
        hidden = gated_unit(gate_value, lift_value).astype(jnp.bfloat16)
        output = (stream_two + project(hidden, down_full)).astype(jnp.bfloat16)
        back_weights = (
            lax.all_gather(weight_shards[0], ("dp", "seq"), axis=0, tiled=True),
            lax.all_gather(weight_shards[1], ("dp", "seq"), axis=0, tiled=True),
            lax.all_gather(weight_shards[2], ("dp", "seq"), axis=0, tiled=True),
            lax.all_gather(weight_shards[3], ("dp", "seq"), axis=0, tiled=True),
            lax.all_gather(weight_shards[4], ("dp", "seq"), axis=0, tiled=True),
            lax.all_gather(weight_shards[5], ("dp", "seq"), axis=0, tiled=True),
            lax.all_gather(weight_shards[6], ("dp", "seq"), axis=0, tiled=True),
            lax.all_gather(weight_shards[7], ("dp", "seq"), axis=0, tiled=True),
            lax.all_gather(weight_shards[8], ("dp", "seq"), axis=0, tiled=True),
            lax.all_gather(weight_shards[9], ("dp", "seq"), axis=0, tiled=True),
            lax.all_gather(weight_shards[10], ("dp", "seq"), axis=0, tiled=True),
            lax.all_gather(weight_shards[11], ("dp", "seq"), axis=0, tiled=True),
            lax.all_gather(weight_shards[12], ("dp", "seq"), axis=0, tiled=True),
            lax.all_gather(weight_shards[13], ("dp", "seq"), axis=0, tiled=True),
            lax.all_gather(weight_shards[14], ("dp", "seq"), axis=0, tiled=True),
        )
        (
            query_back,
            key_back,
            value_back,
            output_back,
            cquery_back,
            ckey_back,
            cvalue_back,
            coutput_back,
            gate_back,
            lift_back,
            down_back,
            first_back,
            second_back,
            third_back,
            table_back,
        ) = back_weights
        grad_stream = cot_in[None].astype(jnp.float32)
        low_down = cot_in[None]
        grad_down = weight_grad(hidden, low_down)
        grad_hidden = project_back(low_down, down_back)
        grad_gate, grad_lift = jax.vjp(gated_unit, gate_value, lift_value)[1](grad_hidden)
        low_gate = grad_gate.astype(jnp.bfloat16)
        low_lift = grad_lift.astype(jnp.bfloat16)
        grad_gate_weight = weight_grad(act_third, low_gate)
        grad_lift_weight = weight_grad(act_third, low_lift)
        grad_act = project_back(low_gate, gate_back) + project_back(low_lift, lift_back)
        grad_norm, grad_gain_third = jax.vjp(rms_scale, stream_two, third_back.astype(jnp.float32))[
            1
        ](grad_act)
        grad_stream = grad_stream + grad_norm
        low_branch = grad_stream.astype(jnp.bfloat16)
        grad_output_cross = weight_grad(cross_att, low_branch)
        grad_cross_att = (
            project_back(low_branch, coutput_back)
            .astype(jnp.bfloat16)
            .reshape(1, local_span, G, per_group, HD)
        )
        cross_again = jnp.exp(
            logits_of(cross_queries, cross_keys, 0.0, cross_allowed, scaling) - cross_lse
        )
        unused_logits, grad_cq, grad_ck, grad_cv = attention_back(
            cross_again, cross_queries, cross_keys, cross_values, grad_cross_att, scaling
        )
        cross_kv_grad = jnp.concatenate(
            [grad_ck.reshape(1, mem_total, kv_width), grad_cv.reshape(1, mem_total, kv_width)],
            axis=-1,
        )
        memory_kv_grad = lax.psum_scatter(
            cross_kv_grad.astype(jnp.bfloat16), "seq", scatter_dimension=1, tiled=True
        )
        grad_kv_cross = weight_grad(mem_block, memory_kv_grad)
        memory_grad = project_back(
            memory_kv_grad, jnp.concatenate([ckey_back, cvalue_back], axis=1)
        )
        low_cq = grad_cq.reshape(1, local_span, H * HD).astype(jnp.bfloat16)
        grad_query_cross = weight_grad(act_second, low_cq)
        grad_act = project_back(low_cq, cquery_back)
        grad_norm, grad_gain_second = jax.vjp(
            rms_scale, stream_one, second_back.astype(jnp.float32)
        )[1](grad_act)
        grad_stream = grad_stream + grad_norm
        low_branch = grad_stream.astype(jnp.bfloat16)
        grad_output_self = weight_grad(self_att, low_branch)
        grad_self_att = (
            project_back(low_branch, output_back)
            .astype(jnp.bfloat16)
            .reshape(1, local_span, G, per_group, HD)
        )
        self_again = jnp.exp(
            logits_of(query_heads, self_keys, self_bias, causal, scaling) - self_lse
        )
        grad_logits, grad_sq, grad_sk, grad_sv = attention_back(
            self_again, query_heads, self_keys, self_values, grad_self_att, scaling
        )
        grad_table = jnp.einsum(
            "hpl,bpl->bh",
            jnp.sum(grad_logits, axis=0).reshape(H, local_span, full_length),
            one_hot.astype(jnp.float32),
            precision=highest,
        ).reshape(NB * H)
        self_kv_grad = jnp.concatenate(
            [grad_sk.reshape(1, full_length, kv_width), grad_sv.reshape(1, full_length, kv_width)],
            axis=-1,
        )
        local_kv_grad = lax.psum_scatter(
            self_kv_grad.astype(jnp.bfloat16), "seq", scatter_dimension=1, tiled=True
        )
        low_sq = grad_sq.reshape(1, local_span, H * HD).astype(jnp.bfloat16)
        grad_query_self = weight_grad(act_first, low_sq)
        grad_kv_self = weight_grad(act_first, local_kv_grad)
        grad_act = project_back(low_sq, query_back) + project_back(
            local_kv_grad, jnp.concatenate([key_back, value_back], axis=1)
        )
        grad_norm, grad_gain_first = jax.vjp(rms_scale, stream, first_back.astype(jnp.float32))[1](
            grad_act
        )
        input_grad = grad_stream + grad_norm
        grads = (
            grad_query_self,
            grad_kv_self[:, :kv_width],
            grad_kv_self[:, kv_width:],
            grad_output_self,
            grad_query_cross,
            grad_kv_cross[:, :kv_width],
            grad_kv_cross[:, kv_width:],
            grad_output_cross,
            grad_gate_weight,
            grad_lift_weight,
            grad_down,
            grad_gain_first,
            grad_gain_second,
            grad_gain_third,
            grad_table,
        )
        return ((output[0], input_grad[0], memory_grad[0]), grads)

    elements = (inputs, memory, mem_lengths, cross_mask, cotangent)

    def step_each(carry, element):
        results, grads = micro(element)
        summed = (
            lax.psum_scatter(grads[0], ("dp", "seq"), scatter_dimension=0, tiled=True),
            lax.psum_scatter(grads[1], ("dp", "seq"), scatter_dimension=0, tiled=True),
            lax.psum_scatter(grads[2], ("dp", "seq"), scatter_dimension=0, tiled=True),
            lax.psum_scatter(grads[3], ("dp", "seq"), scatter_dimension=0, tiled=True),
            lax.psum_scatter(grads[4], ("dp", "seq"), scatter_dimension=0, tiled=True),
            lax.psum_scatter(grads[5], ("dp", "seq"), scatter_dimension=0, tiled=True),
            lax.psum_scatter(grads[6], ("dp", "seq"), scatter_dimension=0, tiled=True),
            lax.psum_scatter(grads[7], ("dp", "seq"), scatter_dimension=0, tiled=True),
            lax.psum_scatter(grads[8], ("dp", "seq"), scatter_dimension=0, tiled=True),
            lax.psum_scatter(grads[9], ("dp", "seq"), scatter_dimension=0, tiled=True),
            lax.psum_scatter(grads[10], ("dp", "seq"), scatter_dimension=0, tiled=True),
            lax.psum_scatter(grads[11], ("dp", "seq"), scatter_dimension=0, tiled=True),
            lax.psum_scatter(grads[12], ("dp", "seq"), scatter_dimension=0, tiled=True),
            lax.psum_scatter(grads[13], ("dp", "seq"), scatter_dimension=0, tiled=True),
            lax.psum_scatter(grads[14], ("dp", "seq"), scatter_dimension=0, tiled=True),
        )
        return (tuple((held + added for held, added in zip(carry, summed))), results)

    start = tuple((jnp.zeros(shard.shape, jnp.float32) for shard in weight_shards))
    totals, (output, input_grad, memory_grad) = lax.scan(step_each, start, elements)
    return (
        output,
        input_grad,
        memory_grad,
        totals[0],
        totals[1],
        totals[2],
        totals[3],
        totals[4],
        totals[5],
        totals[6],
        totals[7],
        totals[8],
        totals[9],
        totals[10],
        totals[11],
        totals[12],
        totals[13],
        totals[14],
    )


def solution(mesh):
    placed = (
        P("dp", "seq", None),
        P("dp", "seq", None),
        P("dp"),
        P("dp", None),
        P(),
        P(("dp", "seq"), None),
        P(("dp", "seq"), None),
        P(("dp", "seq"), None),
        P(("dp", "seq"), None),
        P(("dp", "seq"), None),
        P(("dp", "seq"), None),
        P(("dp", "seq"), None),
        P(("dp", "seq"), None),
        P(("dp", "seq"), None),
        P(("dp", "seq"), None),
        P(("dp", "seq"), None),
        P(("dp", "seq")),
        P(("dp", "seq")),
        P(("dp", "seq")),
        P(("dp", "seq")),
        P("dp", "seq", None),
    )
    return jax.shard_map(
        shards,
        mesh=mesh,
        in_specs=placed,
        out_specs=(
            P("dp", "seq", None),
            P("dp", "seq", None),
            P("dp", "seq", None),
            P(("dp", "seq"), None),
            P(("dp", "seq"), None),
            P(("dp", "seq"), None),
            P(("dp", "seq"), None),
            P(("dp", "seq"), None),
            P(("dp", "seq"), None),
            P(("dp", "seq"), None),
            P(("dp", "seq"), None),
            P(("dp", "seq"), None),
            P(("dp", "seq"), None),
            P(("dp", "seq"), None),
            P(("dp", "seq")),
            P(("dp", "seq")),
            P(("dp", "seq")),
            P(("dp", "seq")),
        ),
        check_vma=False,
    )
```

profile of v0, /device:TPU:0, one launch (start us, length us, event | category | flops | bytes accessed | tf_op | source)
XLA Modules:
  0.0 5409.3 jit_solution(17517269840416163539)
XLA Ops:
  7.9 520.8 %gather_fusion = s32[131072]{0:T(1024)S(1)} fusion(s32[1024]{0:T(1024)S(1)} %copy-done, s32[131072]{0:T(1024)S(1)} %broadcast_clamp_fusion), kind=kCustom, calls=%fused_computation | custom fusion | bytes 1572864 | tf_op jit(solution)/shard_map/jit(_take)/gather | solution.py:132
  530.1 4871.6 %while.47 = (s32[]{:T(128)}, f32[32,1024]{1,0:T(8,128)}, f32[32,512]{1,0:T(8,128)}, f32[32,512]{1,0:T(8,128)}, f32[32,1024]{1,0:T(8,128)}, /*index=5*/f32[32,102...) while((s32[]{:T(128)}, f32[32,1024]{1,0:T(8,128)}, ...), condition=%wide.region_33.34_spmd.clone, body=%wide.region_0.33_spmd.clone.sunk | while | flops 14534331392 | bytes 899993536 | solution.py:390
  533.4 57.5 %all-gather.32.cloned.1.call-done = bf16[1024,512]{1,0:T(8,128)(2,1)} async-done(((bf16[32,512]{1,0:T(8,128)(2,1)}), bf16[1024,512]{1,0:T(8,128)(2,1)}) %all-gather.32.cloned.1.call-update) | async-done | bytes 1048592 | tf_op jit(solution)/shard_map/while/body/eval_jaxpr/all_gather | solution.py:148
  930.6 56.2 %all-gather.38.cloned.1.call-done = bf16[1024,1024]{1,0:T(8,128)(2,1)} async-done(((bf16[32,1024]{1,0:T(8,128)(2,1)}), bf16[1024,1024]{1,0:T(8,128)(2,1)}) %all-gather.38.cloned.1.call-update) | async-done | bytes 2097168 | tf_op jit(solution)/shard_map/while/body/eval_jaxpr/all_gather | solution.py:147
  1047.8 66.2 %all-gather.44.cloned.1.call-done = bf16[2816,1024]{1,0:T(8,128)(2,1)} async-done(((bf16[88,1024]{1,0:T(8,128)(2,1)}), bf16[2816,1024]{1,0:T(8,128)(2,1)}) %all-gather.44.cloned.1.call-update) | async-done | bytes 5767184 | tf_op jit(solution)/shard_map/while/body/eval_jaxpr/all_gather | solution.py:243
  1119.9 63.1 %all-gather.42.cloned.1.call-done = bf16[1024,2816]{1,0:T(8,128)(2,1)} async-done(((bf16[32,2816]{1,0:T(8,128)(2,1)}), bf16[1024,2816]{1,0:T(8,128)(2,1)}) %all-gather.42.cloned.1.call-update) | async-done | bytes 5767184 | tf_op jit(solution)/shard_map/while/body/eval_jaxpr/all_gather | solution.py:151
  1187.8 64.4 %all-gather.46.cloned.1.call-done = bf16[1024,2816]{1,0:T(8,128)(2,1)} async-done(((bf16[32,2816]{1,0:T(8,128)(2,1)}), bf16[1024,2816]{1,0:T(8,128)(2,1)}) %all-gather.46.cloned.1.call-update) | async-done | bytes 5767184 | tf_op jit(solution)/shard_map/while/body/eval_jaxpr/all_gather | solution.py:152
  1513.4 134.5 %reduce-scatter.38.cloned.1.call-done = f32[32,512]{1,0:T(8,128)} async-done(((f32[1024,512]{1,0:T(8,128)}), f32[32,512]{1,0:T(8,128)}) %reduce-scatter.38.cloned.1.call-update) | async-done | bytes 65552 | tf_op jit(solution)/shard_map/while/body/eval_jaxpr/reduce_scatter | solution.py:377
  1648.7 134.2 %reduce-scatter.26.cloned.1.call-done = f32[32,512]{1,0:T(8,128)} async-done(((f32[1024,512]{1,0:T(8,128)}), f32[32,512]{1,0:T(8,128)}) %reduce-scatter.26.cloned.1.call-update) | async-done | bytes 65552 | tf_op jit(solution)/shard_map/while/body/eval_jaxpr/reduce_scatter | solution.py:372
  1783.8 135.2 %reduce-scatter.28.cloned.1.call-done = f32[32,512]{1,0:T(8,128)} async-done(((f32[1024,512]{1,0:T(8,128)}), f32[32,512]{1,0:T(8,128)}) %reduce-scatter.28.cloned.1.call-update) | async-done | bytes 65552 | tf_op jit(solution)/shard_map/while/body/eval_jaxpr/reduce_scatter | solution.py:373
  1919.8 140.9 %reduce-scatter.32.cloned.1.call-done = f32[32,1024]{1,0:T(8,128)} async-done(((f32[1024,1024]{1,0:T(8,128)}), f32[32,1024]{1,0:T(8,128)}) %reduce-scatter.32.cloned.1.call-update) | async-done | bytes 131088 | tf_op jit(solution)/shard_map/while/body/eval_jaxpr/reduce_scatter | solution.py:375
  2061.7 140.8 %reduce-scatter.40.cloned.1.call-done = f32[32,1024]{1,0:T(8,128)} async-done(((f32[1024,1024]{1,0:T(8,128)}), f32[32,1024]{1,0:T(8,128)}) %reduce-scatter.40.cloned.1.call-update) | async-done | bytes 131088 | tf_op jit(solution)/shard_map/while/body/eval_jaxpr/reduce_scatter | solution.py:378
  2203.5 140.8 %reduce-scatter.30.cloned.1.call-done = f32[32,1024]{1,0:T(8,128)} async-done(((f32[1024,1024]{1,0:T(8,128)}), f32[32,1024]{1,0:T(8,128)}) %reduce-scatter.30.cloned.1.call-update) | async-done | bytes 131088 | tf_op jit(solution)/shard_map/while/body/eval_jaxpr/reduce_scatter | solution.py:374
  2345.2 141.1 %reduce-scatter.22.cloned.1.call-done = f32[32,1024]{1,0:T(8,128)} async-done(((f32[1024,1024]{1,0:T(8,128)}), f32[32,1024]{1,0:T(8,128)}) %reduce-scatter.22.cloned.1.call-update) | async-done | bytes 131088 | tf_op jit(solution)/shard_map/while/body/eval_jaxpr/reduce_scatter | solution.py:371
  2487.3 159.1 %reduce-scatter.46.cloned.1.call-done = f32[88,1024]{1,0:T(8,128)} async-done(((f32[2816,1024]{1,0:T(8,128)}), f32[88,1024]{1,0:T(8,128)}) %reduce-scatter.46.cloned.1.call-update) | async-done | bytes 360464 | tf_op jit(solution)/shard_map/while/body/eval_jaxpr/reduce_scatter | solution.py:381
  2647.5 159.2 %reduce-scatter.44.cloned.1.call-done = f32[32,2816]{1,0:T(8,128)} async-done(((f32[1024,2816]{1,0:T(8,128)}), f32[32,2816]{1,0:T(8,128)}) %reduce-scatter.44.cloned.1.call-update) | async-done | bytes 360464 | tf_op jit(solution)/shard_map/while/body/eval_jaxpr/reduce_scatter | solution.py:380
  2807.8 159.8 %reduce-scatter.42.cloned.1.call-done = f32[32,2816]{1,0:T(8,128)} async-done(((f32[1024,2816]{1,0:T(8,128)}), f32[32,2816]{1,0:T(8,128)}) %reduce-scatter.42.cloned.1.call-update) | async-done | bytes 360464 | tf_op jit(solution)/shard_map/while/body/eval_jaxpr/reduce_scatter | solution.py:379
  3026.7 54.4 %all-gather.34.cloned.1.call-done = bf16[1024,512]{1,0:T(8,128)(2,1)} async-done(((bf16[32,512]{1,0:T(8,128)(2,1)}), bf16[1024,512]{1,0:T(8,128)(2,1)}) %all-gather.34.cloned.1.call-update) | async-done | bytes 1048592 | tf_op jit(solution)/shard_map/while/body/eval_jaxpr/all_gather | solution.py:149
  3365.2 56.2 %all-gather.38.cloned.1.call-done = bf16[1024,1024]{1,0:T(8,128)(2,1)} async-done(((bf16[32,1024]{1,0:T(8,128)(2,1)}), bf16[1024,1024]{1,0:T(8,128)(2,1)}) %all-gather.38.cloned.1.call-update) | async-done | bytes 2097168 | tf_op jit(solution)/shard_map/while/body/eval_jaxpr/all_gather | solution.py:147
  3482.4 66.1 %all-gather.44.cloned.1.call-done = bf16[2816,1024]{1,0:T(8,128)(2,1)} async-done(((bf16[88,1024]{1,0:T(8,128)(2,1)}), bf16[2816,1024]{1,0:T(8,128)(2,1)}) %all-gather.44.cloned.1.call-update) | async-done | bytes 5767184 | tf_op jit(solution)/shard_map/while/body/eval_jaxpr/all_gather | solution.py:243
  3554.3 63.3 %all-gather.42.cloned.1.call-done = bf16[1024,2816]{1,0:T(8,128)(2,1)} async-done(((bf16[32,2816]{1,0:T(8,128)(2,1)}), bf16[1024,2816]{1,0:T(8,128)(2,1)}) %all-gather.42.cloned.1.call-update) | async-done | bytes 5767184 | tf_op jit(solution)/shard_map/while/body/eval_jaxpr/all_gather | solution.py:151
  3622.3 64.3 %all-gather.46.cloned.1.call-done = bf16[1024,2816]{1,0:T(8,128)(2,1)} async-done(((bf16[32,2816]{1,0:T(8,128)(2,1)}), bf16[1024,2816]{1,0:T(8,128)(2,1)}) %all-gather.46.cloned.1.call-update) | async-done | bytes 5767184 | tf_op jit(solution)/shard_map/while/body/eval_jaxpr/all_gather | solution.py:152
  3948.5 134.0 %reduce-scatter.38.cloned.1.call-done = f32[32,512]{1,0:T(8,128)} async-done(((f32[1024,512]{1,0:T(8,128)}), f32[32,512]{1,0:T(8,128)}) %reduce-scatter.38.cloned.1.call-update) | async-done | bytes 65552 | tf_op jit(solution)/shard_map/while/body/eval_jaxpr/reduce_scatter | solution.py:377
  4083.3 134.7 %reduce-scatter.26.cloned.1.call-done = f32[32,512]{1,0:T(8,128)} async-done(((f32[1024,512]{1,0:T(8,128)}), f32[32,512]{1,0:T(8,128)}) %reduce-scatter.26.cloned.1.call-update) | async-done | bytes 65552 | tf_op jit(solution)/shard_map/while/body/eval_jaxpr/reduce_scatter | solution.py:372
  4218.9 134.4 %reduce-scatter.28.cloned.1.call-done = f32[32,512]{1,0:T(8,128)} async-done(((f32[1024,512]{1,0:T(8,128)}), f32[32,512]{1,0:T(8,128)}) %reduce-scatter.28.cloned.1.call-update) | async-done | bytes 65552 | tf_op jit(solution)/shard_map/while/body/eval_jaxpr/reduce_scatter | solution.py:373
  4354.2 139.8 %reduce-scatter.32.cloned.1.call-done = f32[32,1024]{1,0:T(8,128)} async-done(((f32[1024,1024]{1,0:T(8,128)}), f32[32,1024]{1,0:T(8,128)}) %reduce-scatter.32.cloned.1.call-update) | async-done | bytes 131088 | tf_op jit(solution)/shard_map/while/body/eval_jaxpr/reduce_scatter | solution.py:375
  4494.9 140.5 %reduce-scatter.40.cloned.1.call-done = f32[32,1024]{1,0:T(8,128)} async-done(((f32[1024,1024]{1,0:T(8,128)}), f32[32,1024]{1,0:T(8,128)}) %reduce-scatter.40.cloned.1.call-update) | async-done | bytes 131088 | tf_op jit(solution)/shard_map/while/body/eval_jaxpr/reduce_scatter | solution.py:378
  4636.3 141.3 %reduce-scatter.30.cloned.1.call-done = f32[32,1024]{1,0:T(8,128)} async-done(((f32[1024,1024]{1,0:T(8,128)}), f32[32,1024]{1,0:T(8,128)}) %reduce-scatter.30.cloned.1.call-update) | async-done | bytes 131088 | tf_op jit(solution)/shard_map/while/body/eval_jaxpr/reduce_scatter | solution.py:374
  4778.6 140.4 %reduce-scatter.22.cloned.1.call-done = f32[32,1024]{1,0:T(8,128)} async-done(((f32[1024,1024]{1,0:T(8,128)}), f32[32,1024]{1,0:T(8,128)}) %reduce-scatter.22.cloned.1.call-update) | async-done | bytes 131088 | tf_op jit(solution)/shard_map/while/body/eval_jaxpr/reduce_scatter | solution.py:371
  4919.9 158.6 %reduce-scatter.46.cloned.1.call-done = f32[88,1024]{1,0:T(8,128)} async-done(((f32[2816,1024]{1,0:T(8,128)}), f32[88,1024]{1,0:T(8,128)}) %reduce-scatter.46.cloned.1.call-update) | async-done | bytes 360464 | tf_op jit(solution)/shard_map/while/body/eval_jaxpr/reduce_scatter | solution.py:381
  5079.6 159.0 %reduce-scatter.44.cloned.1.call-done = f32[32,2816]{1,0:T(8,128)} async-done(((f32[1024,2816]{1,0:T(8,128)}), f32[32,2816]{1,0:T(8,128)}) %reduce-scatter.44.cloned.1.call-update) | async-done | bytes 360464 | tf_op jit(solution)/shard_map/while/body/eval_jaxpr/reduce_scatter | solution.py:380
  5239.7 159.1 %reduce-scatter.42.cloned.1.call-done = f32[32,2816]{1,0:T(8,128)} async-done(((f32[1024,2816]{1,0:T(8,128)}), f32[32,2816]{1,0:T(8,128)}) %reduce-scatter.42.cloned.1.call-update) | async-done | bytes 360464 | tf_op jit(solution)/shard_map/while/body/eval_jaxpr/reduce_scatter | solution.py:379
  (661 shorter events, 1370.5 us)
Async XLA Ops:
  533.4 247.5 %all-gather.36.cloned.1.call-start = ((), (), s32[]{:S(2)}) async-start(), calls=%async_computation.20 | async-start | bytes 1179648 | tf_op jit(solution)/shard_map/while/body/eval_jaxpr/all_gather | solution.py:187
  765.0 280.0 %all-gather.40.cloned.1.call-start = ((), (), s32[]{:S(2)}) async-start(), calls=%async_computation.22 | async-start | bytes 2162688 | tf_op jit(solution)/shard_map/while/body/eval_jaxpr/all_gather | solution.py:150
  765.6 348.4 %all-gather.44.cloned.1.call-start = ((), (), s32[]{:S(2)}) async-start(), calls=%async_computation.24 | async-start | bytes 5947392 | tf_op jit(solution)/shard_map/while/body/eval_jaxpr/all_gather | solution.py:243
  766.3 416.7 %all-gather.42.cloned.1.call-start = ((), (), s32[]{:S(2)}) async-start(), calls=%async_computation.23 | async-start | bytes 5947392 | tf_op jit(solution)/shard_map/while/body/eval_jaxpr/all_gather | solution.py:151
  766.9 485.3 %all-gather.46.cloned.1.call-start = ((), (), s32[]{:S(2)}) async-start(), calls=%async_computation.25 | async-start | bytes 5947392 | tf_op jit(solution)/shard_map/while/body/eval_jaxpr/all_gather | solution.py:152
  767.7 571.9 %reduce-scatter.34.cloned.1.call-start = ((), (), s32[]{:S(2)}) async-start(), calls=%async_computation.32 | async-start | bytes 1179648 | tf_op jit(solution)/shard_map/while
  1347.5 300.3 %reduce-scatter.38.cloned.1.call-start = ((), (), s32[]{:S(2)}) async-start(), calls=%async_computation.34 | async-start | bytes 2162688 | tf_op jit(solution)/shard_map/while/body/eval_jaxpr/reduce_scatter | solution.py:377
  1348.1 434.8 %reduce-scatter.26.cloned.1.call-start = ((), (), s32[]{:S(2)}) async-start(), calls=%async_computation.28 | async-start | bytes 2162688 | tf_op jit(solution)/shard_map/while/body/eval_jaxpr/reduce_scatter | solution.py:372
  1382.7 536.2 %reduce-scatter.28.cloned.1.call-start = ((), (), s32[]{:S(2)}) async-start(), calls=%async_computation.29 | async-start | bytes 2162688 | tf_op jit(solution)/shard_map/while/body/eval_jaxpr/reduce_scatter | solution.py:373
  1383.5 677.3 %reduce-scatter.32.cloned.1.call-start = ((), (), s32[]{:S(2)}) async-start(), calls=%async_computation.31 | async-start | bytes 4325376 | tf_op jit(solution)/shard_map/while/body/eval_jaxpr/reduce_scatter | solution.py:375
  1387.3 815.2 %reduce-scatter.40.cloned.1.call-start = ((), (), s32[]{:S(2)}) async-start(), calls=%async_computation.35 | async-start | bytes 4325376 | tf_op jit(solution)/shard_map/while/body/eval_jaxpr/reduce_scatter | solution.py:378
  1391.2 953.1 %reduce-scatter.30.cloned.1.call-start = ((), (), s32[]{:S(2)}) async-start(), calls=%async_computation.30 | async-start | bytes 4325376 | tf_op jit(solution)/shard_map/while/body/eval_jaxpr/reduce_scatter | solution.py:374
  1395.0 1091.3 %reduce-scatter.22.cloned.1.call-start = ((), (), s32[]{:S(2)}) async-start(), calls=%async_computation.26 | async-start | bytes 4325376 | tf_op jit(solution)/shard_map/while/body/eval_jaxpr/reduce_scatter | solution.py:371
  1404.1 1242.3 %reduce-scatter.46.cloned.1.call-start = ((), (), s32[]{:S(2)}) async-start(), calls=%async_computation.38 | async-start | bytes 11894784 | tf_op jit(solution)/shard_map/while/body/eval_jaxpr/reduce_scatter | solution.py:381
  1411.2 1395.5 %reduce-scatter.44.cloned.1.call-start = ((), (), s32[]{:S(2)}) async-start(), calls=%async_computation.37 | async-start | bytes 11894784 | tf_op jit(solution)/shard_map/while/body/eval_jaxpr/reduce_scatter | solution.py:380
  1418.3 1549.3 %reduce-scatter.42.cloned.1.call-start = ((), (), s32[]{:S(2)}) async-start(), calls=%async_computation.36 | async-start | bytes 11894784 | tf_op jit(solution)/shard_map/while/body/eval_jaxpr/reduce_scatter | solution.py:379
  2972.5 243.0 %all-gather.36.cloned.1.call-start = ((), (), s32[]{:S(2)}) async-start(), calls=%async_computation.20 | async-start | bytes 1179648 | tf_op jit(solution)/shard_map/while/body/eval_jaxpr/all_gather | solution.py:187
  3199.4 280.2 %all-gather.40.cloned.1.call-start = ((), (), s32[]{:S(2)}) async-start(), calls=%async_computation.22 | async-start | bytes 2162688 | tf_op jit(solution)/shard_map/while/body/eval_jaxpr/all_gather | solution.py:150
  3200.0 348.5 %all-gather.44.cloned.1.call-start = ((), (), s32[]{:S(2)}) async-start(), calls=%async_computation.24 | async-start | bytes 5947392 | tf_op jit(solution)/shard_map/while/body/eval_jaxpr/all_gather | solution.py:243
  3200.6 417.1 %all-gather.42.cloned.1.call-start = ((), (), s32[]{:S(2)}) async-start(), calls=%async_computation.23 | async-start | bytes 5947392 | tf_op jit(solution)/shard_map/while/body/eval_jaxpr/all_gather | solution.py:151
  3201.3 485.3 %all-gather.46.cloned.1.call-start = ((), (), s32[]{:S(2)}) async-start(), calls=%async_computation.25 | async-start | bytes 5947392 | tf_op jit(solution)/shard_map/while/body/eval_jaxpr/all_gather | solution.py:152
  3201.9 572.1 %reduce-scatter.34.cloned.1.call-start = ((), (), s32[]{:S(2)}) async-start(), calls=%async_computation.32 | async-start | bytes 1179648 | tf_op jit(solution)/shard_map/while
  3782.0 300.5 %reduce-scatter.38.cloned.1.call-start = ((), (), s32[]{:S(2)}) async-start(), calls=%async_computation.34 | async-start | bytes 2162688 | tf_op jit(solution)/shard_map/while/body/eval_jaxpr/reduce_scatter | solution.py:377
  3782.5 435.5 %reduce-scatter.26.cloned.1.call-start = ((), (), s32[]{:S(2)}) async-start(), calls=%async_computation.28 | async-start | bytes 2162688 | tf_op jit(solution)/shard_map/while/body/eval_jaxpr/reduce_scatter | solution.py:372
  3817.1 536.2 %reduce-scatter.28.cloned.1.call-start = ((), (), s32[]{:S(2)}) async-start(), calls=%async_computation.29 | async-start | bytes 2162688 | tf_op jit(solution)/shard_map/while/body/eval_jaxpr/reduce_scatter | solution.py:373
  3817.7 676.3 %reduce-scatter.32.cloned.1.call-start = ((), (), s32[]{:S(2)}) async-start(), calls=%async_computation.31 | async-start | bytes 4325376 | tf_op jit(solution)/shard_map/while/body/eval_jaxpr/reduce_scatter | solution.py:375
  3821.5 813.9 %reduce-scatter.40.cloned.1.call-start = ((), (), s32[]{:S(2)}) async-start(), calls=%async_computation.35 | async-start | bytes 4325376 | tf_op jit(solution)/shard_map/while/body/eval_jaxpr/reduce_scatter | solution.py:378
  3825.4 952.2 %reduce-scatter.30.cloned.1.call-start = ((), (), s32[]{:S(2)}) async-start(), calls=%async_computation.30 | async-start | bytes 4325376 | tf_op jit(solution)/shard_map/while/body/eval_jaxpr/reduce_scatter | solution.py:374
  3829.2 1089.7 %reduce-scatter.22.cloned.1.call-start = ((), (), s32[]{:S(2)}) async-start(), calls=%async_computation.26 | async-start | bytes 4325376 | tf_op jit(solution)/shard_map/while/body/eval_jaxpr/reduce_scatter | solution.py:371
  3838.2 1240.2 %reduce-scatter.46.cloned.1.call-start = ((), (), s32[]{:S(2)}) async-start(), calls=%async_computation.38 | async-start | bytes 11894784 | tf_op jit(solution)/shard_map/while/body/eval_jaxpr/reduce_scatter | solution.py:381
  3845.4 1393.2 %reduce-scatter.44.cloned.1.call-start = ((), (), s32[]{:S(2)}) async-start(), calls=%async_computation.37 | async-start | bytes 11894784 | tf_op jit(solution)/shard_map/while/body/eval_jaxpr/reduce_scatter | solution.py:380
  3852.5 1546.3 %reduce-scatter.42.cloned.1.call-start = ((), (), s32[]{:S(2)}) async-start(), calls=%async_computation.36 | async-start | bytes 11894784 | tf_op jit(solution)/shard_map/while/body/eval_jaxpr/reduce_scatter | solution.py:379
  (156 other events, 45533.4 us)
Sparse Core Ops, SparseCore 0:
  534.4 56.4 all-gather.31
  783.8 56.0 all-gather.27
  1047.9 66.1 all-gather.43
  1116.8 66.2 all-gather.41
  1185.9 66.2 all-gather.45
  1376.5 135.2 reduce-scatter.35
  1514.1 133.7 reduce-scatter.37
  1650.0 132.8 reduce-scatter.25
  1785.2 133.6 reduce-scatter.27
  1921.1 139.6 reduce-scatter.31
  2063.0 139.4 reduce-scatter.39
  2204.8 139.4 reduce-scatter.29
  2346.6 139.7 reduce-scatter.21
  2488.5 157.8 reduce-scatter.45
  2648.7 157.9 reduce-scatter.43
  2808.9 158.7 reduce-scatter.41
  3218.4 56.0 all-gather.27
  3307.0 55.9 all-gather.29
  3482.3 66.1 all-gather.43
  3551.3 66.2 all-gather.41
  3620.3 66.2 all-gather.45
  3811.0 135.8 reduce-scatter.35
  3949.1 133.2 reduce-scatter.37
  4084.7 133.2 reduce-scatter.25
  4220.3 132.9 reduce-scatter.27
  4355.4 138.4 reduce-scatter.31
  4496.1 139.2 reduce-scatter.39
  4637.5 140.0 reduce-scatter.29
  4779.7 139.1 reduce-scatter.21
  4921.2 157.1 reduce-scatter.45
  5080.6 157.9 reduce-scatter.43
  5240.9 157.8 reduce-scatter.41
  (20 shorter events, 874.9 us)
where the time goes:
time: 5420 us; the launch traced here: 5410 us
  waiting for transfers between devices  4200 us (77%)
  local copies, waits for them, and re-layouts  674 us (12%)
  matrix products  298 us (5%)
  blocking collectives  156 us (3%)
  other arithmetic  62.6 us (1%)
    gather x2, local copies, waits for them, and re-layouts, shards(): bucket_index = jnp.take(buckets, jnp.clip(distance, 0, full_length - 1))  521 us
    reduce_scatter x2, waiting for transfers between devices, step_each(): lax.psum_scatter(grads[8], ('dp', 'seq'), scatter_dimension=0, tiled=True)  319 us
    reduce_scatter x2, waiting for transfers between devices, step_each(): lax.psum_scatter(grads[9], ('dp', 'seq'), scatter_dimension=0, tiled=True)  318 us
    reduce_scatter x2, waiting for transfers between devices, step_each(): lax.psum_scatter(grads[10], ('dp', 'seq'), scatter_dimension=0, tiled=True)  318 us
    reduce_scatter x2, waiting for transfers between devices, step_each(): lax.psum_scatter(grads[3], ('dp', 'seq'), scatter_dimension=0, tiled=True)  282 us
    reduce_scatter x2, waiting for transfers between devices, step_each(): lax.psum_scatter(grads[0], ('dp', 'seq'), scatter_dimension=0, tiled=True)  281 us
    reduce_scatter x2, waiting for transfers between devices, step_each(): lax.psum_scatter(grads[7], ('dp', 'seq'), scatter_dimension=0, tiled=True)  281 us
    reduce_scatter x2, waiting for transfers between devices, step_each(): lax.psum_scatter(grads[4], ('dp', 'seq'), scatter_dimension=0, tiled=True)  281 us
  transfers between devices with their start and end apart: 52, of which 50 were waited for; matrix products, arithmetic and copies ran while one was open for 8% of the time, Pallas kernels for 0%

commit v1 on v0

v1 whole, which is shorter than its diff:
```python
import functools

import jax
import jax.numpy as jnp
from jax import lax
from jax.experimental import pallas as pl
from jax.experimental.pallas import tpu as pltpu
from jax.sharding import PartitionSpec as P

H = 16
HD = 64
NB = 32
G = 8
PER = H // G

epsilon = 1e-06
highest = lax.Precision.HIGHEST
masked_out = -1e30
bf16 = jnp.bfloat16
f32 = jnp.float32
LANES = 128


def layout():
    dp, seq = lax.axis_size("dp"), lax.axis_size("seq")
    return {
        "y": ("dp", dp // 2, 2),
        "x": ("dp", 1, dp // 2),
        "z": ("seq", 2, seq // 2),
        "c": ("seq", 1, 2),
    }


def my_digit(digit):
    axis, stride, size = digit
    return (lax.axis_index(axis) // stride) % size


def hop(value, digit):
    axis, stride, size = digit
    pairs = []
    for source in range(lax.axis_size(axis)):
        mine = (source // stride) % size
        pairs.append((source, source + ((mine + 1) % size - mine) * stride))
    return lax.ppermute(value, axis, pairs)


def gather_digit(value, digit, at):
    size, mine = digit[2], my_digit(digit)
    if size == 1:
        return jnp.expand_dims(value, at)
    if size == 2:
        other = hop(value, digit)
        upper = mine == 1
        return jnp.stack(
            [jnp.where(upper, other, value), jnp.where(upper, value, other)], axis=at
        )
    held = [value]
    for _ in range(size - 1):
        held.append(hop(held[-1], digit))
    turned = jnp.stack(held[::-1] + held[::-1], axis=at)
    return lax.dynamic_slice_in_dim(turned, size - 1 - mine, size, axis=at)


def reduce_digit(value, digit, at, kind=bf16):
    size, mine = digit[2], my_digit(digit)

    def piece(back):
        return lax.dynamic_index_in_dim(
            value, (mine - 1 - back + 2 * size) % size, at, keepdims=False
        )

    if size == 1:
        return jnp.squeeze(value, at).astype(kind)
    total = piece(0)
    for step in range(1, size):
        total = hop(total, digit).astype(f32) + piece(step).astype(f32)
        total = total.astype(kind if step == size - 1 else value.dtype)
    return total


def gather_all(shard, x_first):
    d = layout()
    held = gather_digit(shard, d["z"], 0)
    if x_first:
        held = gather_digit(gather_digit(held, d["x"], 0), d["y"], 0)
    else:
        held = gather_digit(gather_digit(held, d["y"], 0), d["x"], 1)
    held = gather_digit(held, d["c"], 3)
    return held.reshape((-1,) + shard.shape)


def scatter_all(value, x_last):
    d = layout()
    held = value.reshape(tuple(d[k][2] for k in "yxzc") + value.shape[1:])
    held = reduce_digit(held, d["c"], 3)
    if x_last:
        held = reduce_digit(reduce_digit(held, d["y"], 0), d["x"], 0)
    else:
        held = reduce_digit(reduce_digit(held, d["x"], 1), d["y"], 0)
    return reduce_digit(held, d["z"], 0, f32)


def heads_of(block, group):
    low = PER * group * HD
    return jnp.concatenate([block[:, low : low + HD], block[:, low + HD : low + 2 * HD]], axis=0)


def nt(left, right):
    return lax.dot_general(left, right, (((1,), (1,)), ((), ())), preferred_element_type=f32)


def attention_forward_kernel(causal, pad, start_ref, q_ref, k_ref, v_ref, b_ref, o_ref, p_ref):
    span = q_ref.shape[1]
    keys = k_ref[...].reshape(-1, LANES)
    values = v_ref[...].reshape(-1, LANES)
    queries = q_ref[0]
    length = keys.shape[0]
    for group in range(2):
        key_rows = keys[:, group * HD : (group + 1) * HD]
        value_rows = values[:, group * HD : (group + 1) * HD]
        scores = nt(heads_of(queries, group), key_rows) * HD ** (-0.5)
        if causal:
            tiles = []
            for head in (2 * group, 2 * group + 1):
                base = jnp.broadcast_to(b_ref[0, head : head + 1, :], (span, b_ref.shape[2]))
                tiles.append(pltpu.roll(base, 0, 1, stride=1, stride_axis=0)[:, pad:])
            row = lax.broadcasted_iota(jnp.int32, (span, length), 0) + start_ref[0]
            ahead = lax.broadcasted_iota(jnp.int32, (span, length), 1) > row
            tiles = [jnp.where(ahead, masked_out, tile) for tile in tiles]
            scores = scores + jnp.concatenate(tiles, axis=0)
        else:
            scores = scores + b_ref[0]
        peak = jnp.max(scores, axis=1, keepdims=True)
        exps = jnp.exp(scores - peak)
        probs = (exps * (1.0 / jnp.sum(exps, axis=1, keepdims=True))).astype(bf16)
        mixed = jnp.dot(probs, value_rows, preferred_element_type=f32).astype(bf16)
        for half in range(2):
            head = 2 * group + half
            p_ref[0, head] = probs[half * span : (half + 1) * span]
            o_ref[0, :, head * HD : (head + 1) * HD] = mixed[half * span : (half + 1) * span]


def sum_diagonals(tile):
    rows, width = tile.shape
    while rows > 1:
        rows //= 2
        tile = tile[:rows] + pltpu.roll(tile[rows:], width - rows, 1)
    return tile


def attention_backward_kernel(causal, pad, q_ref, k_ref, v_ref, g_ref, p_ref, *outs):
    dq_ref, dk_ref, dv_ref = outs[:3]
    span = q_ref.shape[1]
    keys = k_ref[...].reshape(-1, LANES)
    values = v_ref[...].reshape(-1, LANES)
    queries, grads = q_ref[0], g_ref[0]
    length = keys.shape[0]
    scaling = HD ** (-0.5)
    down_k, down_v = [], []
    for group in range(2):
        key_rows = keys[:, group * HD : (group + 1) * HD]
        value_rows = values[:, group * HD : (group + 1) * HD]
        query_rows = heads_of(queries, group)
        grad_rows = heads_of(grads, group)
        low_probs = p_ref[0, 2 * group : 2 * group + 2].reshape(2 * span, length)
        probs = low_probs.astype(f32)
        grad_probs = nt(grad_rows, value_rows)
        mean = jnp.sum(probs * grad_probs, axis=1, keepdims=True)
        grad_logits = probs * (grad_probs - mean)
        low = grad_logits.astype(bf16)
        dq = (jnp.dot(low, key_rows, preferred_element_type=f32) * scaling).astype(bf16)
        for half in range(2):
            head = 2 * group + half
            dq_ref[0, :, head * HD : (head + 1) * HD] = dq[half * span : (half + 1) * span]
        flat_q = query_rows.astype(f32).T.astype(bf16)
        flat_g = grad_rows.astype(f32).T.astype(bf16)
        down_k.append(jnp.dot(flat_q, low, preferred_element_type=f32) * scaling)
        down_v.append(jnp.dot(flat_g, low_probs, preferred_element_type=f32))
        if causal:
            for half in range(2):
                head = 2 * group + half
                tile = grad_logits[half * span : (half + 1) * span]
                wide = jnp.concatenate([jnp.zeros((span, pad), f32), tile], axis=1)
                outs[3][0, head : head + 1, :] = sum_diagonals(wide)
    dk_ref[...] = jnp.concatenate(down_k, axis=0).T.astype(bf16).reshape(dk_ref.shape)
    dv_ref[...] = jnp.concatenate(down_v, axis=0).T.astype(bf16).reshape(dv_ref.shape)


def attention_specs(queries, kv, bias):
    seqs, span, width = queries.shape
    blocks, _, rows, _ = kv.shape
    steps = width // (4 * HD)
    q_spec = pl.BlockSpec((1, span, 4 * HD), lambda s, j, *_: (s, 0, j))
    k_spec = pl.BlockSpec((blocks, 1, rows, LANES), lambda s, j, *_: (0, s, 0, j))
    v_spec = pl.BlockSpec((blocks, 1, rows, LANES), lambda s, j, *_: (0, s, 0, steps + j))
    p_spec = pl.BlockSpec((1, 4, span, blocks * rows), lambda s, j, *_: (s, j, 0, 0))
    return (seqs, steps), q_spec, k_spec, v_spec, p_spec


def attention_forward(queries, kv, bias, start, causal, pad):
    seqs, span, width = queries.shape
    length = kv.shape[0] * kv.shape[2]
    grid, q_spec, k_spec, v_spec, p_spec = attention_specs(queries, kv, bias)
    if causal:
        b_spec = pl.BlockSpec((1,) + bias.shape[1:], lambda s, j, *_: (j, 0, 0))
    else:
        b_spec = pl.BlockSpec((1,) + bias.shape[1:], lambda s, j, *_: (s, 0, 0))
    ops = seqs * H * span * length
    return pl.pallas_call(
        functools.partial(attention_forward_kernel, causal, pad),
        out_shape=(
            jax.ShapeDtypeStruct(queries.shape, bf16),
            jax.ShapeDtypeStruct((seqs, H, span, length), bf16),
        ),
        grid_spec=pltpu.PrefetchScalarGridSpec(
            num_scalar_prefetch=1,
            grid=grid,
            in_specs=[q_spec, k_spec, v_spec, b_spec],
            out_specs=(q_spec, p_spec),
        ),
        compiler_params=pltpu.CompilerParams(vmem_limit_bytes=40 << 20),
        cost_estimate=pl.CostEstimate(
            flops=4 * ops * HD, bytes_accessed=2 * ops, transcendentals=ops
        ),
        name="attend_causal" if causal else "attend_memory",
    )(start, queries, kv, kv, bias)


def attention_backward(queries, kv, grads, probs, causal, pad):
    seqs, span, width = queries.shape
    length = kv.shape[0] * kv.shape[2]
    grid, q_spec, k_spec, v_spec, p_spec = attention_specs(queries, kv, None)
    kv_out = jax.ShapeDtypeStruct(kv.shape[:3] + (G * HD,), bf16)
    kv_out_spec = k_spec
    out_shape = [jax.ShapeDtypeStruct(queries.shape, bf16), kv_out, kv_out]
    out_specs = [q_spec, kv_out_spec, kv_out_spec]
    if causal:
        out_shape.append(jax.ShapeDtypeStruct((seqs * grid[1], 4, pad + length), f32))
        steps = grid[1]
        out_specs.append(
            pl.BlockSpec((1, 4, pad + length), lambda s, j: (s * steps + j, 0, 0))
        )
    ops = seqs * H * span * length
    return pl.pallas_call(
        functools.partial(attention_backward_kernel, causal, pad),
        out_shape=out_shape,
        grid=grid,
        in_specs=[q_spec, k_spec, v_spec, q_spec, p_spec],
        out_specs=out_specs,
        compiler_params=pltpu.CompilerParams(vmem_limit_bytes=48 << 20),
        cost_estimate=pl.CostEstimate(flops=8 * ops * HD, bytes_accessed=2 * ops, transcendentals=0),
        name="attend_causal_back" if causal else "attend_memory_back",
    )(queries, kv, kv, grads, probs)


def rms_scale(stream, norm_gain):
    return (
        stream * lax.rsqrt(jnp.mean(stream * stream, axis=-1, keepdims=True) + epsilon) * norm_gain
    )


def gated_unit(gate_value, lift_value):
    return jax.nn.gelu(gate_value, approximate=True) * lift_value


def project(left, right):
    return jnp.dot(left, right, preferred_element_type=f32)


def project_back(left, right):
    return nt(left, right)


def weight_grad(left, right):
    return lax.dot_general(left, right, (((0,), (0,)), ((), ())), preferred_element_type=f32)


def shards(
    inputs,
    memory,
    mem_lengths,
    cross_mask,
    buckets,
    self_query,
    self_key,
    self_value,
    self_output,
    cross_query,
    cross_key,
    cross_value,
    cross_output,
    gate_weight,
    up_weight,
    down_weight,
    self_gain,
    cross_gain,
    feed_gain,
    position_bias,
    cotangent,
):
    seqs, span, width = inputs.shape
    mem_span = memory.shape[1]
    seq_count = lax.axis_size("seq")
    devices = seq_count * lax.axis_size("dp")
    length = span * seq_count
    mem_total = mem_span * seq_count
    rows = self_query.shape[0]
    kv_width = G * HD
    tokens = seqs * span
    pad = -(-span // LANES) * LANES
    first_row = lax.axis_index("seq") * span

    small = jnp.concatenate([self_gain, cross_gain, feed_gain, position_bias])
    small_count = small.shape[0]
    small_rows = 8 * -(-small_count // (8 * width))
    small = jnp.pad(small, (0, small_rows * width - small_count)).reshape(small_rows, width)
    part_a = jnp.concatenate(
        [self_query, jnp.concatenate([self_key, self_value], axis=1), small], axis=0
    )
    part_b = jnp.concatenate(
        [
            self_output,
            jnp.concatenate([cross_key, cross_value], axis=1),
            cross_query,
            cross_output,
        ],
        axis=0,
    )
    full_a = gather_all(part_a, True)
    full_b = gather_all(part_b, False)
    gate_full = gather_all(gate_weight, True).reshape(width, -1)
    lift_full = gather_all(up_weight, False).reshape(width, -1)
    down_full = gather_all(down_weight, True).reshape(-1, width)

    def cut(full, at, count=rows):
        return full[:, at : at + count].reshape(devices * count, width)

    query_self, kv_self = cut(full_a, 0), cut(full_a, rows)
    small_full = full_a[:, 2 * rows :].reshape(devices, small_rows * width)[:, :small_count]
    output_self, kv_cross = cut(full_b, 0), cut(full_b, rows)
    query_cross, output_cross = cut(full_b, 2 * rows), cut(full_b, 3 * rows)
    part = self_gain.shape[0]
    gain_first = small_full[:, :part].reshape(-1).astype(f32)
    gain_second = small_full[:, part : 2 * part].reshape(-1).astype(f32)
    gain_third = small_full[:, 2 * part : 3 * part].reshape(-1).astype(f32)
    bias_table = small_full[:, 3 * part :].reshape(NB, H)

    turned = jnp.pad(buckets[::-1], (pad, length), constant_values=-1)
    turned = lax.dynamic_slice(turned, (length - 1 - first_row,), (pad + length,))
    one_hot = turned[None, :] == jnp.arange(NB, dtype=jnp.int32)[:, None]
    terms = jnp.einsum(
        "bh,bc->hc", bias_table, one_hot.astype(bf16), preferred_element_type=f32
    ).reshape(H // 4, 4, pad + length)
    start = jnp.reshape(first_row, (1,)).astype(jnp.int32)

    stream = inputs.reshape(tokens, width).astype(f32)
    mem_block = memory.reshape(seqs * mem_span, width)
    act_first = rms_scale(stream, gain_first).astype(bf16)
    local_kv = project(act_first, kv_self).astype(bf16).reshape(seqs, span, 2 * kv_width)
    full_kv = lax.all_gather(local_kv, "seq", axis=0)
    memory_kv = project(mem_block, kv_cross).astype(bf16).reshape(seqs, mem_span, 2 * kv_width)
    full_memory_kv = lax.all_gather(memory_kv, "seq", axis=0)
    queries = project(act_first, query_self).astype(bf16).reshape(seqs, span, H * HD)
    self_att, self_probs = attention_forward(queries, full_kv, terms, start, True, pad)
    flat_self = self_att.reshape(tokens, H * HD)
    stream_one = stream + project(flat_self, output_self)
    act_second = rms_scale(stream_one, gain_second).astype(bf16)
    cross_queries = project(act_second, query_cross).astype(bf16).reshape(seqs, span, H * HD)
    usable = (cross_mask > 0) & (
        jnp.arange(mem_total, dtype=jnp.int32)[None, :] < mem_lengths[:, None]
    )
    shut = jnp.where(usable, 0.0, masked_out).astype(f32)[:, None, :]
    cross_att, cross_probs = attention_forward(
        cross_queries, full_memory_kv, shut, start, False, pad
    )
    flat_cross = cross_att.reshape(tokens, H * HD)
    stream_two = stream_one + project(flat_cross, output_cross)
    act_third = rms_scale(stream_two, gain_third).astype(bf16)
    gate_value = project(act_third, gate_full)
    lift_value = project(act_third, lift_full)
    hidden = gated_unit(gate_value, lift_value).astype(bf16)
    output = (stream_two + project(hidden, down_full)).astype(bf16)

    low_down = cotangent.reshape(tokens, width)
    grad_stream = low_down.astype(f32)
    grad_down = weight_grad(hidden, low_down).astype(bf16)
    grad_hidden = project_back(low_down, down_full)
    grad_gate, grad_lift = jax.vjp(gated_unit, gate_value, lift_value)[1](grad_hidden)
    low_gate = grad_gate.astype(bf16)
    low_lift = grad_lift.astype(bf16)
    grad_gate_weight = weight_grad(act_third, low_gate).astype(bf16)
    grad_lift_weight = weight_grad(act_third, low_lift).astype(bf16)

    def by_device(grad):
        return grad.reshape(devices, -1, grad.shape[-1])

    down_total = scatter_all(by_device(grad_down), True)
    gate_total = scatter_all(by_device(grad_gate_weight), False)
    lift_total = scatter_all(by_device(grad_lift_weight), True)

    grad_act = project_back(low_gate, gate_full) + project_back(low_lift, lift_full)
    grad_norm, grad_gain_third = jax.vjp(rms_scale, stream_two, gain_third)[1](grad_act)
    grad_stream = grad_stream + grad_norm
    low_branch = grad_stream.astype(bf16)
    grad_output_cross = weight_grad(flat_cross, low_branch).astype(bf16)
    grad_cross_att = project_back(low_branch, output_cross).astype(bf16)
    grad_cq, grad_ck, grad_cv = attention_backward(
        cross_queries,
        full_memory_kv,
        grad_cross_att.reshape(seqs, span, H * HD),
        cross_probs,
        False,
        pad,
    )
    memory_kv_grad = lax.psum_scatter(
        jnp.concatenate([grad_ck, grad_cv], axis=-1), "seq", scatter_dimension=0
    ).reshape(seqs * mem_span, 2 * kv_width)
    grad_kv_cross = weight_grad(mem_block, memory_kv_grad).astype(bf16)
    memory_grad = project_back(memory_kv_grad, kv_cross)
    low_cq = grad_cq.reshape(tokens, H * HD)
    grad_query_cross = weight_grad(act_second, low_cq).astype(bf16)
    grad_act = project_back(low_cq, query_cross)
    grad_norm, grad_gain_second = jax.vjp(rms_scale, stream_one, gain_second)[1](grad_act)
    grad_stream = grad_stream + grad_norm
    low_branch = grad_stream.astype(bf16)
    grad_output_self = weight_grad(flat_self, low_branch).astype(bf16)
    total_b = scatter_all(
        jnp.concatenate(
            [
                by_device(g)
                for g in (grad_output_self, grad_kv_cross, grad_query_cross, grad_output_cross)
            ],
            axis=1,
        ),
        False,
    )
    grad_self_att = project_back(low_branch, output_self).astype(bf16)
    grad_sq, grad_sk, grad_sv, diagonals = attention_backward(
        queries, full_kv, grad_self_att.reshape(seqs, span, H * HD), self_probs, True, pad
    )
    grad_table = jnp.einsum(
        "hc,bc->bh",
        jnp.sum(diagonals.reshape(seqs, H, pad + length), axis=0),
        one_hot.astype(f32),
        precision=highest,
    )
    local_kv_grad = lax.psum_scatter(
        jnp.concatenate([grad_sk, grad_sv], axis=-1), "seq", scatter_dimension=0
    ).reshape(tokens, 2 * kv_width)
    low_sq = grad_sq.reshape(tokens, H * HD)
    grad_query_self = weight_grad(act_first, low_sq).astype(bf16)
    grad_kv_self = weight_grad(act_first, local_kv_grad).astype(bf16)
    grad_act = project_back(low_sq, query_self) + project_back(local_kv_grad, kv_self)
    grad_norm, grad_gain_first = jax.vjp(rms_scale, stream, gain_first)[1](grad_act)
    input_grad = grad_stream + grad_norm
    small_grad = jnp.concatenate(
        [
            grad_gain_first.reshape(devices, -1),
            grad_gain_second.reshape(devices, -1),
            grad_gain_third.reshape(devices, -1),
            grad_table.reshape(devices, -1),
        ],
        axis=1,
    )
    small_grad = jnp.pad(small_grad, ((0, 0), (0, small_rows * width - small_count)))
    total_a = scatter_all(
        jnp.concatenate(
            [
                by_device(grad_query_self),
                by_device(grad_kv_self),
                small_grad.astype(bf16).reshape(devices, small_rows, width),
            ],
            axis=1,
        ),
        True,
    )
    small_total = total_a[2 * rows :].reshape(-1)[:small_count]

    def row_block(total, index):
        return total[index * rows : (index + 1) * rows]

    kv_total, cross_kv_total = row_block(total_a, 1), row_block(total_b, 1)
    return (
        output.reshape(inputs.shape),
        input_grad.reshape(inputs.shape),
        memory_grad.reshape(memory.shape),
        row_block(total_a, 0),
        kv_total[:, :kv_width],
        kv_total[:, kv_width:],
        row_block(total_b, 0),
        row_block(total_b, 2),
        cross_kv_total[:, :kv_width],
        cross_kv_total[:, kv_width:],
        row_block(total_b, 3),
        gate_total,
        lift_total,
        down_total,
        small_total[:part],
        small_total[part : 2 * part],
        small_total[2 * part : 3 * part],
        small_total[3 * part :],
    )


def solution(mesh):
    rows_split = P("dp", "seq", None)
    weight_split = P(("dp", "seq"), None)
    vector_split = P(("dp", "seq"))
    return jax.shard_map(
        shards,
        mesh=mesh,
        in_specs=(rows_split, rows_split, P("dp"), P("dp", None), P())
        + (weight_split,) * 11
        + (vector_split,) * 4
        + (rows_split,),
        out_specs=(rows_split,) * 3 + (weight_split,) * 11 + (vector_split,) * 4,
        check_vma=False,
    )
```

time: 5420 us -> 714 us (0.13)
  waiting for transfers between devices: 4200 us -> 345 us
  local copies, waits for them, and re-layouts: 674 us -> 75.4 us
  matrix products: 298 us -> 61.4 us
  blocking collectives: 156 us -> 0 us
  Pallas kernels: 0 us -> 60.7 us
    reduce_scatter x22 -> x2, waiting for transfers between devices: 2930 us -> 0.02 us  [the longest x1 0.02 us: shards(): lax.psum_scatter(jnp.concatenate([grad_sk, grad_sv], axis=-1), 'seq', sca...]
    all_gather x26 -> x2, waiting for transfers between devices: 1200 us -> 0.02 us  [the longest x1 0.02 us: shards(): full_memory_kv = lax.all_gather(memory_kv, 'seq', axis=0)]
    gather x2 -> x0, local copies, waits for them, and re-layouts: 521 us -> none  [shards(): bucket_index = jnp.take(buckets, jnp.clip(distance, 0, full_length - 1))]
    ppermute x0 -> x60, waiting for transfers between devices: none -> 345 us  [hop(): return lax.ppermute(value, axis, pairs)]
    dot_general x82 -> x29, matrix products: 298 us -> 61.4 us  [the longest x9 23.1 us: project(): return jnp.dot(left, right, preferred_element_type=f32)]
    while x4 -> x0, blocking collectives: 156 us -> none
    while x292 -> x0, local copies, waits for them, and re-layouts: 94.3 us -> none
    while x56 -> x0, waiting for transfers between devices: 68.9 us -> none
  transfers between devices with their start and end apart: 52 -> 64, of which waited for: 50 -> 33; matrix products, arithmetic and copies ran while one was open for 8% -> 25% of each run, Pallas kernels for 0% -> 3%
where the time goes in v1:
time: 714 us; the launch traced here: 706 us
  waiting for transfers between devices  345 us (48%)
  other arithmetic  105 us (15%)
  local copies, waits for them, and re-layouts  75.4 us (11%)
  matrix products  61.4 us (9%)
  Pallas kernels  60.7 us (9%)
  starting transfers between devices  42.1 us (6%)
  between operations  16.5 us (2%)
    ppermute x60, waiting for transfers between devices, hop(): return lax.ppermute(value, axis, pairs)  345 us
    another operation x30, other arithmetic, gather_digit(): jnp.stack([jnp.where(upper, other, value), jnp.where(upper, value, other)...  51.8 us
    ppermute x60, starting transfers between devices, hop(): return lax.ppermute(value, axis, pairs)  41 us
    unnamed x274, local copies, waits for them, and re-layouts  37.1 us
    pallas_call x2, Pallas kernels, attention_backward(): pl.pallas_call(functools.partial(attention_backward_kernel, causal, pad),...  32.4 us
    convert_element_type x25, other arithmetic, reduce_digit(): total = total.astype(kind if step == size - 1 else value.dtype)  30 us
    pallas_call x2, Pallas kernels, attention_forward(): pl.pallas_call(functools.partial(attention_forward_kernel, causal, pad),...  28.3 us
    dot_general x9, matrix products, project(): return jnp.dot(left, right, preferred_element_type=f32)  23.1 us
  transfers between devices with their start and end apart: 64, of which 33 were waited for; matrix products, arithmetic and copies ran while one was open for 25% of the time, Pallas kernels for 3%

profile of v1, /device:TPU:0, one launch (start us, length us, event | category | flops | bytes accessed | tf_op | source)
XLA Modules:
  0.0 706.3 jit_solution(4271731202381109387)
XLA Ops:
  30.4 8.7 %collective-permute-done.1 = bf16[72,1024]{1,0:T(8,128)(2,1)S(1)} collective-permute-done((bf16[72,1024]{1,0:T(8,128)(2,1)S(1)}, bf16[72,1024]{1,0:T(8,128)(2,1)S(1)}, u32[]{:S(2)}, u32[]{:S(2)}) %collective-permute-start.1) | collective-permute-done | bytes 147488 | tf_op jit(solution)/shard_map/ppermute | solution.py:45
  59.6 11.6 %collective-permute-done.26 = bf16[88,1024]{1,0:T(8,128)(2,1)S(1)} collective-permute-done((bf16[88,1024]{1,0:T(8,128)(2,1)S(1)}, bf16[88,1024]{1,0:T(8,128)(2,1)S(1)}, u32[]{:S(2)}, u32[]{:S(2)}) %collective-permute-start.26) | collective-permute-done | bytes 180256 | tf_op jit(solution)/shard_map/ppermute | solution.py:45
  79.6 39.2 %collective-permute-done.4 = bf16[2,4,72,1024]{3,2,1,0:T(8,128)(2,1)S(1)} collective-permute-done((bf16[2,4,72,1024]{3,2,1,0:T(8,128)(2,1)S(1)}, bf16[2,4,72,1024]{3,2,1,0:T(8,128)(2,1)S(1)}, u32[]{:S(2)}, u32[]{:S(2)}) %collective-permute-start.4) | collective-permute-done | bytes 1179680 | tf_op jit(solution)/shard_map/ppermute | solution.py:45
  124.1 17.1 %collective-permute-done.9 = bf16[4,128,1024]{2,1,0:T(8,128)(2,1)S(1)} collective-permute-done((bf16[4,128,1024]{2,1,0:T(8,128)(2,1)S(1)}, bf16[4,128,1024]{2,1,0:T(8,128)(2,1)S(1)}, u32[]{:S(2)}, u32[]{:S(2)}) %collective-permute-start.9) | collective-permute-done | bytes 1048608 | tf_op jit(solution)/shard_map/ppermute | solution.py:45
  148.1 4.4 fusion.70
  159.9 42.6 %collective-permute-done.10 = bf16[2,4,128,1024]{3,2,1,0:T(8,128)(2,1)} collective-permute-done((bf16[2,4,128,1024]{3,2,1,0:T(8,128)(2,1)}, bf16[2,4,128,1024]{3,2,1,0:T(8,128)(2,1)}, u32[]{:S(2)}, u32[]{:S(2)}) %collective-permute-start.10) | collective-permute-done | bytes 2097184 | tf_op jit(solution)/shard_map/ppermute | solution.py:45
  218.2 28.6 %collective-permute-done.28 = bf16[2,4,88,1024]{3,2,1,0:T(8,128)(2,1)} collective-permute-done((bf16[2,4,88,1024]{3,2,1,0:T(8,128)(2,1)}, bf16[2,4,88,1024]{3,2,1,0:T(8,128)(2,1)}, u32[]{:S(2)}, u32[]{:S(2)}) %collective-permute-start.28) | collective-permute-done | bytes 1441824 | tf_op jit(solution)/shard_map/ppermute | solution.py:45
  258.6 5.1 select_bitcast_fusion.1
  263.8 7.6 %pad_maximum_fusion = bf16[2,2,4,2,128,1024]{5,4,3,2,1,0:T(8,128)(2,1)} fusion(bf16[2,2,4,1,128,1024]{5,4,3,2,1,0:T(8,128)(2,1)} %get-tuple-element.53, bf16[2,2,4,1,128,1024]{5,4,3,2,1,0:T(8,128)(2,1)} %get-tuple-element.52), kind=kLoop, calls=%fused_computation | loop fusion | flops 4194304 | bytes 16777216 | tf_op jit(solution)/shard_map/stack | solution.py:55
  271.4 5.8 fusion.69
  301.7 19.0 %attend_causal.1 = (bf16[2,128,1024]{2,1,0:T(8,128)(2,1)S(1)}, bf16[2,16,128,1024]{3,2,1,0:T(8,128)(2,1)S(1)}) custom-call(s32[1]{0:T(128)} %bitcast.1.start_ref, bf16[2,128,1024]{2,1,0:T(8,128)(2,1)S(1)} %bitcast.419, bf16[8,2,128,1024]{3,2,1,0:T(8,128)(2,1)S(1)} %copy-done.1, bf16[8,2,128,1024]{3,2,1,0:T(8,128)(2,1)S(1)} %copy-done.1, ...), custom_call_target="tpu_custom_call" | custom-call | flops 1073741824 | bytes 8388608 | tf_op jit(solution)/shard_map/attend_causal/pallas_call | solution.py:210
  328.3 9.3 %attend_memory.1 = (bf16[2,128,1024]{2,1,0:T(8,128)(2,1)S(1)}, bf16[2,16,128,512]{3,2,1,0:T(8,128)(2,1)S(1)}) custom-call(s32[1]{0:T(128)} %bitcast.1.start_ref, bf16[2,128,1024]{2,1,0:T(8,128)(2,1)S(1)} %bitcast.408, bf16[8,2,64,1024]{3,2,1,0:T(8,128)(2,1)S(1)} %copy-done.2, bf16[8,2,64,1024]{3,2,1,0:T(8,128)(2,1)S(1)} %copy-done.2, ...), custom_call_target="tpu_custom_call" | custom-call | flops 536870912 | bytes 4194304 | tf_op jit(solution)/shard_map/attend_memory/pallas_call | solution.py:210
  339.8 5.0 fusion.75
  345.4 5.1 fusion.12
  352.3 4.2 convolution_convert_fusion.2
  360.8 11.5 %attend_memory_back.1 = (bf16[2,128,1024]{2,1,0:T(8,128)(2,1)S(1)}, bf16[8,2,64,512]{3,2,1,0:T(8,128)(2,1)S(1)}, bf16[8,2,64,512]{3,2,1,0:T(8,128)(2,1)S(1)}) custom-call(bf16[2,128,1024]{2,1,0:T(8,128)(2,1)S(1)} %bitcast.409, bf16[8,2,64,1024]{3,2,1,0:T(8,128)(2,1)S(1)} %copy-done.3, bf16[8,2,64,1024]{3,2,1,0:T(8,128)(2,1)S(1)} %copy-done.3, ...), custom_call_target="tpu_custom_call" | custom-call | flops 1073741824 | bytes 4194304 | tf_op jit(solution)/shard_map/attend_memory_back/pallas_call | solution.py:245
  376.2 20.9 %attend_causal_back.1 = (bf16[2,128,1024]{2,1,0:T(8,128)(2,1)S(1)}, bf16[8,2,128,512]{3,2,1,0:T(8,128)(2,1)S(1)}, bf16[8,2,128,512]{3,2,1,0:T(8,128)(2,1)S(1)}, f32[8,4,1152]{2,1,0:T(4,128)S(1)}) custom-call(bf16[2,128,1024]{2,1,0:T(8,128)(2,1)S(1)} %bitcast.420, bf16[8,2,128,1024]{3,2,1,0:T(8,128)(2,1)} %all-gather.3.cloned.1.call-done.k_ref.v_ref, ...), custom_call_target="tpu_custom_call" | custom-call | flops 2147483648 | bytes 8388608 | tf_op jit(solution)/shard_map/attend_causal_back/pallas_call | solution.py:245
  403.4 4.7 constant_dynamic-slice_fusion
  431.0 5.4 fusion.21
  463.0 7.1 %pad_maximum_fusion.1 = bf16[2,2,4,2,128,1024]{5,4,3,2,1,0:T(8,128)(2,1)S(1)} fusion(bf16[2,2,4,2,32,1024]{5,4,3,2,1,0:T(8,128)(2,1)S(1)} %bitcast.449, bf16[2,2,4,2,32,1024]{5,4,3,2,1,0:T(8,128)(2,1)} %bitcast.450, bf16[2,2,4,2,32,1024]{5,4,3,2,1,0:T(8,128)(2,1)S(1)} %bitcast.451, bf16[2,2,4,2,32,1024]{5,4,3,2,1,0:T(8,128)(2,1)S(1)} %bitcast.448), kind=kLoop, calls=%fused_computation.1 | loop fusion | flops 33554432 | bytes 16777216 | tf_op jit(solution)/shard_map/concatenate | solution.py:429
  490.7 28.2 %collective-permute-done.55 = bf16[2,4,88,1024]{3,2,1,0:T(8,128)(2,1)} collective-permute-done((bf16[2,4,88,1024]{3,2,1,0:T(8,128)(2,1)}, bf16[2,4,88,1024]{3,2,1,0:T(8,128)(2,1)}, u32[]{:S(2)}, u32[]{:S(2)}) %collective-permute-start.55) | collective-permute-done | bytes 1441824 | tf_op jit(solution)/shard_map/ppermute | solution.py:45
  521.9 11.9 %collective-permute-done.44 = bf16[4,32,2816]{2,1,0:T(8,128)(2,1)S(1)} collective-permute-done((bf16[4,32,2816]{2,1,0:T(8,128)(2,1)S(1)}, bf16[4,32,2816]{2,1,0:T(8,128)(2,1)S(1)}, u32[]{:S(2)}, u32[]{:S(2)}) %collective-permute-start.44) | collective-permute-done | bytes 720928 | tf_op jit(solution)/shard_map/ppermute | solution.py:45
  538.7 4.7 collective-permute-done.45
  560.8 4.4 fusion
  574.4 5.9 collective-permute-done.59
  581.8 29.9 %collective-permute-done.37 = bf16[2,4,128,1024]{3,2,1,0:T(8,128)(2,1)S(1)} collective-permute-done((bf16[2,4,128,1024]{3,2,1,0:T(8,128)(2,1)S(1)}, bf16[2,4,128,1024]{3,2,1,0:T(8,128)(2,1)S(1)}, u32[]{:S(2)}, u32[]{:S(2)}) %collective-permute-start.37) | collective-permute-done | bytes 2097184 | tf_op jit(solution)/shard_map/ppermute | solution.py:45
  617.0 21.9 %collective-permute-done.38 = bf16[4,128,1024]{2,1,0:T(8,128)(2,1)S(1)} collective-permute-done((bf16[4,128,1024]{2,1,0:T(8,128)(2,1)S(1)}, bf16[4,128,1024]{2,1,0:T(8,128)(2,1)S(1)}, u32[]{:S(2)}, u32[]{:S(2)}) %collective-permute-start.38) | collective-permute-done | bytes 1048608 | tf_op jit(solution)/shard_map/ppermute | solution.py:45
  639.5 21.5 %collective-permute-done.31 = bf16[2,4,72,1024]{3,2,1,0:T(8,128)(2,1)S(1)} collective-permute-done((bf16[2,4,72,1024]{3,2,1,0:T(8,128)(2,1)S(1)}, bf16[2,4,72,1024]{3,2,1,0:T(8,128)(2,1)S(1)}, u32[]{:S(2)}, u32[]{:S(2)}) %collective-permute-start.31) | collective-permute-done | bytes 1179680 | tf_op jit(solution)/shard_map/ppermute | solution.py:45
  663.8 6.9 collective-permute-done.40
  673.9 5.1 collective-permute-done.41
  682.3 7.6 %collective-permute-done.34 = bf16[72,1024]{1,0:T(8,128)(2,1)S(1)} collective-permute-done((bf16[72,1024]{1,0:T(8,128)(2,1)S(1)}, bf16[72,1024]{1,0:T(8,128)(2,1)S(1)}, u32[]{:S(2)}, u32[]{:S(2)}) %collective-permute-start.34) | collective-permute-done | bytes 147488 | tf_op jit(solution)/shard_map/ppermute | solution.py:45
  690.7 6.3 collective-permute-done.35
  (551 shorter events, 272.5 us)
Async XLA Ops:
  7.2 292.3 %all-gather.3.cloned.1.call-start = ((), (), s32[]{:S(2)}) async-start(), calls=%async_computation.2 | async-start | bytes 4718592 | tf_op jit(solution)/shard_map/all_gather | solution.py:361
  43.0 32.9 %collective-permute-start.14 = (bf16[32,2816]{1,0:T(8,128)(2,1)S(1)}, bf16[32,2816]{1,0:T(8,128)(2,1)S(1)}, u32[]{:S(2)}, u32[]{:S(2)}) collective-permute-start(bf16[32,2816]{1,0:T(8,128)(2,1)S(1)} %collective-permute-done.13), channel_id=1, source_target_pairs={{0,2},{1,3},{2,4},{3,5},{4,6},{5,7},{6,0},{7,1},{8,10},{9,11},{10,... | collective-permute-start | bytes 540680 | tf_op jit(solution)/shard_map/ppermute | solution.py:45
  46.9 27.2 %collective-permute-start.20 = (bf16[32,2816]{1,0:T(8,128)(2,1)S(1)}, bf16[32,2816]{1,0:T(8,128)(2,1)S(1)}, u32[]{:S(2)}, u32[]{:S(2)}) collective-permute-start(bf16[32,2816]{1,0:T(8,128)(2,1)S(1)} %collective-permute-done.19), channel_id=1, source_target_pairs={{0,2},{1,3},{2,4},{3,5},{4,6},{5,7},{6,0},{7,1},{8,10},{9,11},{10,... | collective-permute-start | bytes 540680 | tf_op jit(solution)/shard_map/ppermute | solution.py:45
  72.3 137.3 %collective-permute-start.27 = (bf16[4,88,1024]{2,1,0:T(8,128)(2,1)}, bf16[4,88,1024]{2,1,0:T(8,128)(2,1)}, u32[]{:S(2)}, u32[]{:S(2)}) collective-permute-start(bf16[4,88,1024]{2,1,0:T(8,128)(2,1)} %constant_dynamic-slice_fusion.4), channel_id=1, source_target_pairs={{0,8},{8,0},{16,24},{24,16},{1,9},{9,1},{17,25},{25,17},{2,10},{10... | collective-permute-start | bytes 2162696 | tf_op jit(solution)/shard_map/ppermute | solution.py:45
  74.3 47.9 %collective-permute-start.21 = (bf16[4,32,2816]{2,1,0:T(8,128)(2,1)S(1)}, bf16[4,32,2816]{2,1,0:T(8,128)(2,1)S(1)}, u32[]{:S(2)}, u32[]{:S(2)}) collective-permute-start(bf16[4,32,2816]{2,1,0:T(8,128)(2,1)S(1)} %constant_dynamic-slice_fusion.5), channel_id=1, source_target_pairs={{0,16},{8,24},{16,0},{24,8},{1,17},{9,25},{17,1},{25,9},{2,18},{10... | collective-permute-start | bytes 2162696 | tf_op jit(solution)/shard_map/ppermute | solution.py:45
  76.2 43.1 %collective-permute-start.15 = (bf16[4,32,2816]{2,1,0:T(8,128)(2,1)S(1)}, bf16[4,32,2816]{2,1,0:T(8,128)(2,1)S(1)}, u32[]{:S(2)}, u32[]{:S(2)}) collective-permute-start(bf16[4,32,2816]{2,1,0:T(8,128)(2,1)S(1)} %constant_dynamic-slice_fusion.6), channel_id=1, source_target_pairs={{0,8},{8,0},{16,24},{24,16},{1,9},{9,1},{17,25},{25,17},{2,10},{10... | collective-permute-start | bytes 2162696 | tf_op jit(solution)/shard_map/ppermute | solution.py:45
  77.1 41.6 %collective-permute-start.4 = (bf16[2,4,72,1024]{3,2,1,0:T(8,128)(2,1)S(1)}, bf16[2,4,72,1024]{3,2,1,0:T(8,128)(2,1)S(1)}, u32[]{:S(2)}, u32[]{:S(2)}) collective-permute-start(bf16[2,4,72,1024]{3,2,1,0:T(8,128)(2,1)S(1)} %pad_maximum_fusion.18), channel_id=1, source_target_pairs={{0,16},{8,24},{16,0},{24,8},{1,17},{9,25},{17,1},{25,9},{2,18},{10... | collective-permute-start | bytes 3538952 | tf_op jit(solution)/shard_map/ppermute | solution.py:45
  78.1 63.1 %collective-permute-start.9 = (bf16[4,128,1024]{2,1,0:T(8,128)(2,1)S(1)}, bf16[4,128,1024]{2,1,0:T(8,128)(2,1)S(1)}, u32[]{:S(2)}, u32[]{:S(2)}) collective-permute-start(bf16[4,128,1024]{2,1,0:T(8,128)(2,1)S(1)} %constant_dynamic-slice_fusion.7), channel_id=1, source_target_pairs={{0,16},{8,24},{16,0},{24,8},{1,17},{9,25},{17,1},{25,9},{2,18},{10... | collective-permute-start | bytes 3145736 | tf_op jit(solution)/shard_map/ppermute | solution.py:45
  120.7 92.9 %collective-permute-start.16 = (bf16[2,4,32,2816]{3,2,1,0:T(8,128)(2,1)}, bf16[2,4,32,2816]{3,2,1,0:T(8,128)(2,1)}, u32[]{:S(2)}, u32[]{:S(2)}) collective-permute-start(bf16[2,4,32,2816]{3,2,1,0:T(8,128)(2,1)} %pad_maximum_fusion.15), channel_id=1, source_target_pairs={{0,16},{8,24},{16,0},{24,8},{1,17},{9,25},{17,1},{25,9},{2,18},{10... | collective-permute-start | bytes 4325384 | tf_op jit(solution)/shard_map/ppermute | solution.py:45
  123.6 34.7 %collective-permute-start.22 = (bf16[2,4,32,2816]{3,2,1,0:T(8,128)(2,1)}, bf16[2,4,32,2816]{3,2,1,0:T(8,128)(2,1)}, u32[]{:S(2)}, u32[]{:S(2)}) collective-permute-start(bf16[2,4,32,2816]{3,2,1,0:T(8,128)(2,1)} %pad_maximum_fusion.16), channel_id=1, source_target_pairs={{0,8},{8,0},{16,24},{24,16},{1,9},{9,1},{17,25},{25,17},{2,10},{10... | collective-permute-start | bytes 4325384 | tf_op jit(solution)/shard_map/ppermute | solution.py:45
  143.4 59.2 %collective-permute-start.10 = (bf16[2,4,128,1024]{3,2,1,0:T(8,128)(2,1)}, bf16[2,4,128,1024]{3,2,1,0:T(8,128)(2,1)}, u32[]{:S(2)}, u32[]{:S(2)}) collective-permute-start(bf16[2,4,128,1024]{3,2,1,0:T(8,128)(2,1)} %pad_maximum_fusion.13), channel_id=1, source_target_pairs={{0,8},{8,0},{16,24},{24,16},{1,9},{9,1},{17,25},{25,17},{2,10},{10... | collective-permute-start | bytes 6291464 | tf_op jit(solution)/shard_map/ppermute | solution.py:45
  155.3 171.4 %all-gather.5.cloned.1.call-start = ((), (), s32[]{:S(2)}) async-start(), calls=%async_computation.3 | async-start | bytes 2359296 | tf_op jit(solution)/shard_map/all_gather | solution.py:363
  207.3 51.4 %collective-permute-start.11 = (bf16[2,2,4,128,1024]{4,3,2,1,0:T(8,128)(2,1)}, bf16[2,2,4,128,1024]{4,3,2,1,0:T(8,128)(2,1)}, u32[]{:S(2)}, u32[]{:S(2)}) collective-permute-start(bf16[2,2,4,128,1024]{4,3,2,1,0:T(8,128)(2,1)} %pad_maximum_fusion.7), channel_id=1, source_target_pairs={{0,1},{1,0},{2,3},{3,2},{4,5},{5,4},{6,7},{7,6},{8,9},{9,8},{10,11... | collective-permute-start | bytes 12582920 | tf_op jit(solution)/shard_map/ppermute | solution.py:45
  209.1 45.4 %collective-permute-start.23 = (bf16[2,2,4,32,2816]{4,3,2,1,0:T(8,128)(2,1)}, bf16[2,2,4,32,2816]{4,3,2,1,0:T(8,128)(2,1)}, u32[]{:S(2)}, u32[]{:S(2)}) collective-permute-start(bf16[2,2,4,32,2816]{4,3,2,1,0:T(8,128)(2,1)} %pad_maximum_fusion.10), channel_id=1, source_target_pairs={{0,1},{1,0},{2,3},{3,2},{4,5},{5,4},{6,7},{7,6},{8,9},{9,8},{10,11... | collective-permute-start | bytes 8650760 | tf_op jit(solution)/shard_map/ppermute | solution.py:45
  212.9 33.8 %collective-permute-start.28 = (bf16[2,4,88,1024]{3,2,1,0:T(8,128)(2,1)}, bf16[2,4,88,1024]{3,2,1,0:T(8,128)(2,1)}, u32[]{:S(2)}, u32[]{:S(2)}) collective-permute-start(bf16[2,4,88,1024]{3,2,1,0:T(8,128)(2,1)} %pad_maximum_fusion.17), channel_id=1, source_target_pairs={{0,16},{8,24},{16,0},{24,8},{1,17},{9,25},{17,1},{25,9},{2,18},{10... | collective-permute-start | bytes 4325384 | tf_op jit(solution)/shard_map/ppermute | solution.py:45
  218.2 70.7 %collective-permute-start.17 = (bf16[2,2,4,32,2816]{4,3,2,1,0:T(8,128)(2,1)}, bf16[2,2,4,32,2816]{4,3,2,1,0:T(8,128)(2,1)}, u32[]{:S(2)}, u32[]{:S(2)}) collective-permute-start(bf16[2,2,4,32,2816]{4,3,2,1,0:T(8,128)(2,1)} %pad_maximum_fusion.9), channel_id=1, source_target_pairs={{0,1},{1,0},{2,3},{3,2},{4,5},{5,4},{6,7},{7,6},{8,9},{9,8},{10,11... | collective-permute-start | bytes 8650760 | tf_op jit(solution)/shard_map/ppermute | solution.py:45
  250.9 35.2 %collective-permute-start.29 = (bf16[2,2,4,88,1024]{4,3,2,1,0:T(8,128)(2,1)}, bf16[2,2,4,88,1024]{4,3,2,1,0:T(8,128)(2,1)}, u32[]{:S(2)}, u32[]{:S(2)}) collective-permute-start(bf16[2,2,4,88,1024]{4,3,2,1,0:T(8,128)(2,1)} %pad_maximum_fusion.11), channel_id=1, source_target_pairs={{0,1},{1,0},{2,3},{3,2},{4,5},{5,4},{6,7},{7,6},{8,9},{9,8},{10,11... | collective-permute-start | bytes 8650760 | tf_op jit(solution)/shard_map/ppermute | solution.py:45
  279.7 181.4 %reduce-scatter.5.cloned.1.call-start = ((), (), s32[]{:S(2)}) async-start(), calls=%async_computation.5 | async-start | bytes 2359296 | tf_op jit(solution)/shard_map/reduce_scatter | solution.py:416
  403.0 149.1 %reduce-scatter.3.cloned.1.call-start = ((), (), s32[]{:S(2)}) async-start(), calls=%async_computation.4 | async-start | bytes 4718592 | tf_op jit(solution)/shard_map/reduce_scatter | solution.py:448
  409.9 32.7 %collective-permute-start.42 = (bf16[2,2,4,32,2816]{4,3,2,0,1:T(8,128)(2,1)}, bf16[2,2,4,32,2816]{4,3,2,0,1:T(8,128)(2,1)}, u32[]{:S(2)}, u32[]{:S(2)}) collective-permute-start(bf16[2,2,4,32,2816]{4,3,2,0,1:T(8,128)(2,1)} %bitcast.404), channel_id=1, source_target_pairs={{0,1},{1,0},{2,3},{3,2},{4,5},{5,4},{6,7},{7,6},{8,9},{9,8},{10,11... | collective-permute-start | bytes 8650760 | tf_op jit(solution)/shard_map/ppermute | solution.py:45
  415.9 32.3 %collective-permute-start.48 = (bf16[2,2,4,32,2816]{4,3,2,1,0:T(8,128)(2,1)}, bf16[2,2,4,32,2816]{4,3,2,1,0:T(8,128)(2,1)}, u32[]{:S(2)}, u32[]{:S(2)}) collective-permute-start(bf16[2,2,4,32,2816]{4,3,2,1,0:T(8,128)(2,1)} %dynamic-slice_bitcast_fusion.1), channel_id=1, source_target_pairs={{0,1},{1,0},{2,3},{3,2},{4,5},{5,4},{6,7},{7,6},{8,9},{9,8},{10,11... | collective-permute-start | bytes 8650760 | tf_op jit(solution)/shard_map/ppermute | solution.py:45
  421.4 32.3 %collective-permute-start.54 = (bf16[2,2,4,88,1024]{4,3,2,1,0:T(8,128)(2,1)}, bf16[2,2,4,88,1024]{4,3,2,1,0:T(8,128)(2,1)}, u32[]{:S(2)}, u32[]{:S(2)}) collective-permute-start(bf16[2,2,4,88,1024]{4,3,2,1,0:T(8,128)(2,1)} %dynamic-slice_bitcast_fusion), channel_id=1, source_target_pairs={{0,1},{1,0},{2,3},{3,2},{4,5},{5,4},{6,7},{7,6},{8,9},{9,8},{10,11... | collective-permute-start | bytes 8650760 | tf_op jit(solution)/shard_map/ppermute | solution.py:45
  447.7 34.3 %collective-permute-start.43 = (bf16[2,4,32,2816]{3,2,1,0:T(8,128)(2,1)}, bf16[2,4,32,2816]{3,2,1,0:T(8,128)(2,1)}, u32[]{:S(2)}, u32[]{:S(2)}) collective-permute-start(bf16[2,4,32,2816]{3,2,1,0:T(8,128)(2,1)} %dynamic-slice_bitcast_fusion.6), channel_id=1, source_target_pairs={{0,8},{8,0},{16,24},{24,16},{1,9},{9,1},{17,25},{25,17},{2,10},{10... | collective-permute-start | bytes 4325384 | tf_op jit(solution)/shard_map/ppermute | solution.py:45
  453.3 34.7 %collective-permute-start.49 = (bf16[2,4,32,2816]{3,2,1,0:T(8,128)(2,1)}, bf16[2,4,32,2816]{3,2,1,0:T(8,128)(2,1)}, u32[]{:S(2)}, u32[]{:S(2)}) collective-permute-start(bf16[2,4,32,2816]{3,2,1,0:T(8,128)(2,1)} %dynamic-slice_bitcast_fusion.5), channel_id=1, source_target_pairs={{0,16},{8,24},{16,0},{24,8},{1,17},{9,25},{17,1},{25,9},{2,18},{10... | collective-permute-start | bytes 4325384 | tf_op jit(solution)/shard_map/ppermute | solution.py:45
  459.5 59.5 %collective-permute-start.55 = (bf16[2,4,88,1024]{3,2,1,0:T(8,128)(2,1)}, bf16[2,4,88,1024]{3,2,1,0:T(8,128)(2,1)}, u32[]{:S(2)}, u32[]{:S(2)}) collective-permute-start(bf16[2,4,88,1024]{3,2,1,0:T(8,128)(2,1)} %dynamic-slice_bitcast_fusion.4), channel_id=1, source_target_pairs={{0,16},{8,24},{16,0},{24,8},{1,17},{9,25},{17,1},{25,9},{2,18},{10... | collective-permute-start | bytes 4325384 | tf_op jit(solution)/shard_map/ppermute | solution.py:45
  476.2 82.8 %collective-permute-start.36 = (bf16[2,2,4,128,1024]{4,3,2,0,1:T(8,128)(2,1)}, bf16[2,2,4,128,1024]{4,3,2,0,1:T(8,128)(2,1)}, u32[]{:S(2)}, u32[]{:S(2)}) collective-permute-start(bf16[2,2,4,128,1024]{4,3,2,0,1:T(8,128)(2,1)} %bitcast.403), channel_id=1, source_target_pairs={{0,1},{1,0},{2,3},{3,2},{4,5},{5,4},{6,7},{7,6},{8,9},{9,8},{10,11... | collective-permute-start | bytes 12582920 | tf_op jit(solution)/shard_map/ppermute | solution.py:45
  483.8 50.0 %collective-permute-start.44 = (bf16[4,32,2816]{2,1,0:T(8,128)(2,1)S(1)}, bf16[4,32,2816]{2,1,0:T(8,128)(2,1)S(1)}, u32[]{:S(2)}, u32[]{:S(2)}) collective-permute-start(bf16[4,32,2816]{2,1,0:T(8,128)(2,1)S(1)} %dynamic-slice_bitcast_fusion.11), channel_id=1, source_target_pairs={{0,16},{8,24},{16,0},{24,8},{1,17},{9,25},{17,1},{25,9},{2,18},{10... | collective-permute-start | bytes 2162696 | tf_op jit(solution)/shard_map/ppermute | solution.py:45
  489.8 44.3 %collective-permute-start.50 = (bf16[4,32,2816]{2,1,0:T(8,128)(2,1)S(1)}, bf16[4,32,2816]{2,1,0:T(8,128)(2,1)S(1)}, u32[]{:S(2)}, u32[]{:S(2)}) collective-permute-start(bf16[4,32,2816]{2,1,0:T(8,128)(2,1)S(1)} %dynamic-slice_bitcast_fusion.10), channel_id=1, source_target_pairs={{0,8},{8,0},{16,24},{24,16},{1,9},{9,1},{17,25},{25,17},{2,10},{10... | collective-permute-start | bytes 2162696 | tf_op jit(solution)/shard_map/ppermute | solution.py:45
  558.9 54.3 %collective-permute-start.30 = (bf16[2,2,4,72,1024]{4,3,2,1,0:T(8,128)(2,1)S(1)}, bf16[2,2,4,72,1024]{4,3,2,1,0:T(8,128)(2,1)S(1)}, u32[]{:S(2)}, u32[]{:S(2)}) collective-permute-start(bf16[2,2,4,72,1024]{4,3,2,1,0:T(8,128)(2,1)S(1)} %dynamic-slice_bitcast_fusion.2), channel_id=1, source_target_pairs={{0,1},{1,0},{2,3},{3,2},{4,5},{5,4},{6,7},{7,6},{8,9},{9,8},{10,11... | collective-permute-start | bytes 7077896 | tf_op jit(solution)/shard_map/ppermute | solution.py:45
  565.5 46.3 %collective-permute-start.37 = (bf16[2,4,128,1024]{3,2,1,0:T(8,128)(2,1)S(1)}, bf16[2,4,128,1024]{3,2,1,0:T(8,128)(2,1)S(1)}, u32[]{:S(2)}, u32[]{:S(2)}) collective-permute-start(bf16[2,4,128,1024]{3,2,1,0:T(8,128)(2,1)S(1)} %dynamic-slice_bitcast_fusion.3), channel_id=1, source_target_pairs={{0,8},{8,0},{16,24},{24,16},{1,9},{9,1},{17,25},{25,17},{2,10},{10... | collective-permute-start | bytes 6291464 | tf_op jit(solution)/shard_map/ppermute | solution.py:45
  571.2 45.1 %collective-permute-start.53 = (bf16[32,2816]{1,0:T(8,128)(2,1)S(1)}, bf16[32,2816]{1,0:T(8,128)(2,1)S(1)}, u32[]{:S(2)}, u32[]{:S(2)}) collective-permute-start(bf16[32,2816]{1,0:T(8,128)(2,1)S(1)} %fusion.43), channel_id=1, source_target_pairs={{0,2},{1,3},{2,4},{3,5},{4,6},{5,7},{6,0},{7,1},{8,10},{9,11},{10,... | collective-permute-start | bytes 540680 | tf_op jit(solution)/shard_map/ppermute | solution.py:45
  614.5 46.4 %collective-permute-start.31 = (bf16[2,4,72,1024]{3,2,1,0:T(8,128)(2,1)S(1)}, bf16[2,4,72,1024]{3,2,1,0:T(8,128)(2,1)S(1)}, u32[]{:S(2)}, u32[]{:S(2)}) collective-permute-start(bf16[2,4,72,1024]{3,2,1,0:T(8,128)(2,1)S(1)} %dynamic-slice_bitcast_fusion.7), channel_id=1, source_target_pairs={{0,16},{8,24},{16,0},{24,8},{1,17},{9,25},{17,1},{25,9},{2,18},{10... | collective-permute-start | bytes 3538952 | tf_op jit(solution)/shard_map/ppermute | solution.py:45
  (150 other events, 1951.1 us)
Sparse Core Ops, SparseCore 0:
  155.4 46.8 all-gather.2
  279.8 26.8 all-gather.4
  403.1 33.8 reduce-scatter.4
  439.4 49.7 reduce-scatter.2
